TPU v7x, 32 devices: a whole 2x2x4 slice. The times are simulated.
32 devices in a mesh: row: 8 (over y, x, core), col: 4 (over z).
Axes of the slice: x: 2, y: 2, z: 4, core: 2. Of those that a mesh axis runs over, the one named last changes fastest.
Arguments:
- relu21_preact: bfloat16 [256, 256, 128], P('row', 'col'), may hold values from -6 to 6
- relu22_preact: bfloat16 [256, 256, 128], P('row', 'col'), may hold values from -600 to 600
- relu31_preact: bfloat16 [128, 128, 256], P('row', 'col'), may hold values from -6 to 6
- relu32_preact: bfloat16 [128, 128, 256], P('row', 'col'), may hold values from -6 to 6
- relu33_preact: bfloat16 [128, 128, 256], P('row', 'col'), may hold values from -600 to 600
- target22_preact: bfloat16 [256, 256, 128], P('row', 'col'), may hold values from -600 to 600
- target33_preact: bfloat16 [128, 128, 256], P('row', 'col'), may hold values from -600 to 600
- pool1_argmax: int32 [256, 16384], P('row', 'col'), may hold values from 0 to 3
- pool2_argmax: int32 [128, 16384], P('row', 'col'), may hold values from 0 to 3
- linear2_weight: float32 [128], replicated, may hold values from 0.2 to 2
- linear3_weight: float32 [256], replicated, may hold values from 0.2 to 2
- kernel21: bfloat16 [128, 576], replicated, may hold values from -0.25 to 0.25
- kernel22: bfloat16 [128, 1152], replicated, may hold values from -0.1875 to 0.1875
- kernel31: bfloat16 [256, 1152], replicated, may hold values from -0.1875 to 0.1875
- kernel32: bfloat16 [256, 2304], replicated, may hold values from -0.125 to 0.125
- kernel33: bfloat16 [256, 2304], replicated, may hold values from -0.125 to 0.125
Outputs:
- relu12_gradient: bfloat16 [512, 32768], P('row', 'col')
Inputs may be any that keep to these rules, and one draw needn't show every extreme that they name: `pool1_argmax`: the position of the maximum in each 2x2 window, 0 top left, 1 top right, 2 bottom left, 3 bottom right; entry [r, c * 64 + ch] belongs to pooled cell (r, c) and channel ch. `pool2_argmax`: as for pool1_argmax, with 128 channels.
All inputs are finite; a program needn't handle non-finite values.
Results may differ from a plain program's by a relative error of at most 0.0059.
Values may be sent and summed in bfloat16 or wider, within the bound.
A program may use at most 64 MiB of HBM per device.

v0:
```python
import jax
import jax.numpy as jnp
from jax import lax
from jax.sharding import PartitionSpec as P

EPSILON = 1e-06


def extended(cells, sides, width):
    for axis, dim in sides:
        count = lax.axis_size(axis)
        ends = count - 1
        head = lax.slice_in_dim(cells, 0, width, axis=dim)
        tail = lax.slice_in_dim(cells, cells.shape[dim] - width, cells.shape[dim], axis=dim)
        cells = jnp.concatenate(
            [
                lax.ppermute(tail, axis, [(i, (i + 1) % count) for i in range(ends)]),
                cells,
                lax.ppermute(head, axis, [((i + 1) % count, i) for i in range(ends)]),
            ],
            axis=dim,
        )
    return cells


def inject(preact, target, weight):
    feature = jnp.maximum(preact.astype(jnp.float32), 0.0)
    wanted = jnp.maximum(target.astype(jnp.float32), 0.0)
    feature_norm = jnp.sqrt(jnp.mean(feature * feature, axis=-1, keepdims=True) + EPSILON)
    wanted_norm = jnp.sqrt(jnp.mean(wanted * wanted, axis=-1, keepdims=True) + EPSILON)
    scaled = feature / feature_norm
    excess = 2.0 * weight * (scaled - wanted / wanted_norm)
    return (excess - scaled * jnp.mean(excess * scaled, axis=-1, keepdims=True)) / feature_norm


def masked(preact, values):
    return jnp.where(preact > 0, values, 0.0).astype(jnp.bfloat16)


def unpool(values, argmax_rows):
    height, breadth, channels = values.shape
    position = argmax_rows.reshape(height, breadth, channels)
    stripes = []
    for vertical in range(2):
        halves = [
            jnp.where(position == 2 * vertical + lateral, values, 0.0) for lateral in range(2)
        ]
        stripes.append(jnp.stack(halves, axis=2))
    return jnp.stack(stripes, axis=1).reshape(2 * height, 2 * breadth, channels)


def back_conv(padded, kernel):
    out_rows = padded.shape[0] - 2
    out_cols = padded.shape[1] - 2
    amount = kernel.shape[0]
    in_width = kernel.shape[1] // 9
    shifted = [
        padded[
            2 - offset // 3 : 2 - offset // 3 + out_rows, 2 - offset % 3 : 2 - offset % 3 + out_cols
        ]
        for offset in range(9)
    ]
    patches = jnp.stack(shifted, axis=2).reshape(out_rows * out_cols, 9 * amount)
    arranged = kernel.reshape(amount, 9, in_width).transpose(1, 0, 2).reshape(9 * amount, in_width)
    result = jnp.dot(patches, arranged, preferred_element_type=jnp.float32)
    return result.reshape(out_rows, out_cols, in_width)


def shards(
    relu21_preact,
    relu22_preact,
    relu31_preact,
    relu32_preact,
    relu33_preact,
    target22_preact,
    target33_preact,
    pool1_argmax,
    pool2_argmax,
    linear2_weight,
    linear3_weight,
    kernel21,
    kernel22,
    kernel31,
    kernel32,
    kernel33,
):
    seeded = masked(relu33_preact, inject(relu33_preact, target33_preact, linear3_weight))
    border = extended(jnp.stack([relu31_preact, relu32_preact]), (("row", 1), ("col", 2)), 2)
    padded = extended(seeded, (("row", 0), ("col", 1)), 3)
    gradient32 = masked(border[1], back_conv(padded, kernel33))
    gradient31 = masked(border[0, 1:-1, 1:-1], back_conv(gradient32, kernel32))
    pooled2 = back_conv(gradient31, kernel31)
    arriving = unpool(pooled2, pool2_argmax) + inject(
        relu22_preact, target22_preact, linear2_weight
    )
    gradient = masked(relu22_preact, arriving)
    pooled1 = None
    for kernel, preact in ((kernel22, relu21_preact), (kernel21, None)):
        padded = extended(gradient, (("row", 0), ("col", 1)), 1)
        spread = back_conv(padded, kernel)
        if preact is None:
            pooled1 = spread
        else:
            gradient = masked(preact, spread)
    result = unpool(pooled1, pool1_argmax).astype(jnp.bfloat16)
    return result.reshape(result.shape[0], -1)


def solution(mesh):
    in_specs = (
        P("row", "col", None),
        P("row", "col", None),
        P("row", "col", None),
        P("row", "col", None),
        P("row", "col", None),
        P("row", "col", None),
        P("row", "col", None),
        P("row", "col"),
        P("row", "col"),
        P(),
        P(),
        P(),
        P(),
        P(),
        P(),
        P(),
    )
    out_specs = P("row", "col")
    return jax.shard_map(shards, mesh=mesh, in_specs=in_specs, out_specs=out_specs, check_vma=False)
```

profile of v0, /device:TPU:11, one launch (start us, length us, event | category | flops | bytes accessed | tf_op | source)
XLA Modules:
  0.0 102.5 jit_solution(543107133196498689)
XLA Ops:
  0.0 1.2 %multiply_reduce_fusion.4 = f32[16,32]{1,0:T(8,128)S(1)} fusion(bf16[16,32,256]{2,1,0:T(8,128)(2,1)} %param.22), kind=kLoop, calls=%fused_computation.77 | loop fusion | flops 523776 | bytes 264192 | tf_op jit(solution)/shard_map/reduce_sum | solution.py:30
  1.3 1.1 %multiply_reduce_fusion.5 = f32[16,32]{1,0:T(8,128)S(1)} fusion(bf16[16,32,256]{2,1,0:T(8,128)(2,1)} %param.20), kind=kLoop, calls=%fused_computation.80 | loop fusion | flops 523776 | bytes 264192 | tf_op jit(solution)/shard_map/reduce_sum | solution.py:29
  2.4 0.7 broadcast_multiply_fusion.2
  3.1 1.4 %multiply_reduce_fusion.3 = f32[16,32]{1,0:T(8,128)S(1)} fusion(bf16[16,32,256]{2,1,0:T(8,128)(2,1)} %param.20, bf16[16,32,256]{2,1,0:T(8,128)(2,1)} %param.22, f32[16,32]{1,0:T(8,128)S(1)} %get-tuple-element.41, f32[16,32]{1,0:T(8,128)S(1)} %get-tuple-element.42, f32[256]{0:T(256)S(1)} %broadcast_multiply_fusion.2), kind=kLoop, calls=%fused_computation.75 | loop fusion | flops 1310208 | bytes 531456 | tf_op jit(solution)/shard_map/reduce_sum | solution.py:33
  4.5 1.4 %select_convert_fusion.7 = bf16[16,32,256]{2,1,0:T(8,128)(2,1)S(1)} fusion(bf16[16,32,256]{2,1,0:T(8,128)(2,1)} %param.20, bf16[16,32,256]{2,1,0:T(8,128)(2,1)} %param.22, f32[16,32]{1,0:T(8,128)S(1)} %broadcast_multiply_fusion.1, f32[16,32]{1,0:T(8,128)S(1)} %get-tuple-element.41, f32[16,32]{1,0:T(8,128)S(1)} %get-tuple-element.42, ...), kind=kLoop, calls=%fused_computation.74 | loop fusion | flops 1835008 | bytes 793600 | tf_op jit(solution)/shard_map/convert_element_type | solution.py:37
  6.5 3.7 %collective-permute-start.4 = (bf16[3,32,256]{2,1,0:T(8,128)(2,1)}, bf16[3,32,256]{2,1,0:T(8,128)(2,1)}, u32[]{:S(2)}, u32[]{:S(2)}) collective-permute-start(bf16[3,32,256]{2,1,0:T(8,128)(2,1)} %get-tuple-element.39), channel_id=1, source_target_pairs={{0,4},{4,8},{8,12},{12,16},{16,20},{20,24},{24,28},{1,5},{5,9},{9,... | collective-permute-start | bytes 147464 | tf_op jit(solution)/shard_map/ppermute | solution.py:17
  10.2 1.9 %collective-permute-start.5 = (bf16[3,32,256]{2,1,0:T(8,128)(2,1)}, bf16[3,32,256]{2,1,0:T(8,128)(2,1)}, u32[]{:S(2)}, u32[]{:S(2)}) collective-permute-start(bf16[3,32,256]{2,1,0:T(8,128)(2,1)} %get-tuple-element.40), channel_id=1, source_target_pairs={{4,0},{8,4},{12,8},{16,12},{20,16},{24,20},{28,24},{5,1},{9,5},{13... | collective-permute-start | bytes 147464 | tf_op jit(solution)/shard_map/ppermute | solution.py:19
  12.2 1.5 %pad_maximum_fusion.15 = (bf16[2,2,32,256]{3,2,1,0:T(8,128)(2,1)}, bf16[2,2,32,256]{3,2,1,0:T(8,128)(2,1)}) fusion(bf16[1,16,32,256]{3,2,1,0:T(8,128)(2,1)} %bitcast.321, bf16[1,16,32,256]{3,2,1,0:T(8,128)(2,1)} %bitcast.325), kind=kLoop, calls=%fused_computation.156 | loop fusion | flops 65536 | bytes 655360 | tf_op jit(solution)/shard_map/slice | solution.py:14
  13.6 4.5 %collective-permute-start = (bf16[2,2,32,256]{3,2,1,0:T(8,128)(2,1)}, bf16[2,2,32,256]{3,2,1,0:T(8,128)(2,1)}, u32[]{:S(2)}, u32[]{:S(2)}) collective-permute-start(bf16[2,2,32,256]{3,2,1,0:T(8,128)(2,1)} %get-tuple-element.27), channel_id=1, source_target_pairs={{0,4},{4,8},{8,12},{12,16},{16,20},{20,24},{24,28},{1,5},{5,9},{9,... | collective-permute-start | bytes 196616 | tf_op jit(solution)/shard_map/ppermute | solution.py:17
  18.2 1.9 %collective-permute-start.1 = (bf16[2,2,32,256]{3,2,1,0:T(8,128)(2,1)}, bf16[2,2,32,256]{3,2,1,0:T(8,128)(2,1)}, u32[]{:S(2)}, u32[]{:S(2)}) collective-permute-start(bf16[2,2,32,256]{3,2,1,0:T(8,128)(2,1)} %get-tuple-element.28), channel_id=1, source_target_pairs={{4,0},{8,4},{12,8},{16,12},{20,16},{24,20},{28,24},{5,1},{9,5},{13... | collective-permute-start | bytes 196616 | tf_op jit(solution)/shard_map/ppermute | solution.py:19
  20.1 1.1 %compare_bitcast_fusion.3 = (pred[2,8,32,128]{3,1,2,0:T(8,128)(4,1)S(1)}, pred[2,8,32,128]{3,1,2,0:T(8,128)(4,1)S(1)}, pred[2,8,32,128]{3,1,2,0:T(8,128)(4,1)S(1)}, pred[2,8,32,128]{3,1,2,0:T(8,128)(4,1)S(1)}) fusion(s32[16,4096]{1,0:T(8,128)} %param.24), kind=kLoop, calls=%fused_computation.154 | loop fusion | flops 262144 | bytes 524288
  22.0 1.1 %multiply_reduce_fusion = f32[32,64]{1,0:T(8,128)S(1)} fusion(bf16[32,64,128]{2,1,0:T(8,128)(2,1)S(1)} %copy-done.1, bf16[32,64,128]{2,1,0:T(8,128)(2,1)S(1)} %copy-done.2, f32[32,64]{1,0:T(8,128)S(1)} %get-tuple-element.43, f32[32,64]{1,0:T(8,128)S(1)} %get-tuple-element.44, f32[128]{0:T(128)S(1)} %broadcast_multiply_fusion.3), kind=kLoop, calls=%fused_computation.16 | loop fusion | flops 2619392 | bytes 1073664 | tf_op jit(solution)/shard_map/reduce_sum | solution.py:33
  23.6 1.4 %copy.48 = bf16[256,2304]{0,1:T(8,128)(2,1)} copy(bf16[256,2304]{1,0:T(8,128)(2,1)S(1)} %copy-done.3) | data formatting | bytes 2359296 | tf_op args[15]
  25.1 1.6 %copy.50 = bf16[256,2304]{0,1:T(8,128)(2,1)S(1)} copy(bf16[256,2304]{1,0:T(8,128)(2,1)} %param.30) | data formatting | bytes 2359296 | tf_op args[14]
  27.4 0.7 copy.87
  28.0 0.7 copy.88
  28.7 1.3 %copy.53 = bf16[256,1152]{0,1:T(8,128)(2,1)S(1)} copy(bf16[256,1152]{1,0:T(8,128)(2,1)} %param.29) | data formatting | bytes 1179648 | tf_op args[13]
  30.0 0.8 pad_maximum_fusion.18
  30.8 3.2 %collective-permute-start.6 = (bf16[22,3,256]{2,1,0:T(4,128)(2,1)S(1)}, bf16[22,3,256]{2,1,0:T(4,128)(2,1)S(1)}, u32[]{:S(2)}, u32[]{:S(2)}) collective-permute-start(bf16[22,3,256]{2,1,0:T(4,128)(2,1)S(1)} %get-tuple-element.29), channel_id=1, source_target_pairs={{0,1},{1,2},{2,3},{4,5},{5,6},{6,7},{8,9},{9,10},{10,11},{12,13},{... | collective-permute-start | bytes 101384 | tf_op jit(solution)/shard_map/ppermute | solution.py:17
  34.0 2.1 %collective-permute-start.7 = (bf16[22,3,256]{2,1,0:T(4,128)(2,1)S(1)}, bf16[22,3,256]{2,1,0:T(4,128)(2,1)S(1)}, u32[]{:S(2)}, u32[]{:S(2)}) collective-permute-start(bf16[22,3,256]{2,1,0:T(4,128)(2,1)S(1)} %get-tuple-element.30), channel_id=1, source_target_pairs={{1,0},{2,1},{3,2},{5,4},{6,5},{7,6},{9,8},{10,9},{11,10},{13,12},{... | collective-permute-start | bytes 101384 | tf_op jit(solution)/shard_map/ppermute | solution.py:19
  36.2 1.0 pad_maximum_fusion.22
  37.2 3.2 %collective-permute-start.2 = (bf16[2,20,2,256]{3,2,1,0:T(2,128)(2,1)S(1)}, bf16[2,20,2,256]{3,2,1,0:T(2,128)(2,1)S(1)}, u32[]{:S(2)}, u32[]{:S(2)}) collective-permute-start(bf16[2,20,2,256]{3,2,1,0:T(2,128)(2,1)S(1)} %get-tuple-element.5), channel_id=1, source_target_pairs={{0,1},{1,2},{2,3},{4,5},{5,6},{6,7},{8,9},{9,10},{10,11},{12,13},{... | collective-permute-start | bytes 122888 | tf_op jit(solution)/shard_map/ppermute | solution.py:17
  40.4 2.1 %collective-permute-start.3 = (bf16[2,20,2,256]{3,2,1,0:T(2,128)(2,1)S(1)}, bf16[2,20,2,256]{3,2,1,0:T(2,128)(2,1)S(1)}, u32[]{:S(2)}, u32[]{:S(2)}) collective-permute-start(bf16[2,20,2,256]{3,2,1,0:T(2,128)(2,1)S(1)} %get-tuple-element.6), channel_id=1, source_target_pairs={{1,0},{2,1},{3,2},{5,4},{6,5},{7,6},{9,8},{10,9},{11,10},{13,12},{... | collective-permute-start | bytes 122888 | tf_op jit(solution)/shard_map/ppermute | solution.py:19
  42.5 1.1 %pad_maximum_fusion.8 = bf16[22,38,256]{2,1,0:T(8,128)(2,1)S(1)} fusion(bf16[22,3,256]{2,1,0:T(4,128)(2,1)S(1)} %collective-permute-done.7, bf16[3,32,256]{2,1,0:T(8,128)(2,1)} %collective-permute-done.5, bf16[16,32,256]{2,1,0:T(8,128)(2,1)S(1)} %select_convert_fusion.7, bf16[3,32,256]{2,1,0:T(8,128)(2,1)} %collective-permute-done.4, ...), kind=kLoop, calls=%fused_computation.83 | loop fusion | flops 2140160 | bytes 856064 | tf_op jit(solution)/shard_map/concatenate | solution.py:15
  45.1 2.0 %select_convert_fusion.5 = bf16[20,36,256]{2,1,0:T(8,128)(2,1)S(1)} fusion(bf16[2,20,2,256]{3,2,1,0:T(2,128)(2,1)S(1)} %collective-permute-done.3, bf16[2,20,2,256]{3,2,1,0:T(2,128)(2,1)S(1)} %collective-permute-done.2, bf16[2,2,32,256]{3,2,1,0:T(8,128)(2,1)} %collective-permute-done.1, bf16[2,2,32,256]{3,2,1,0:T(8,128)(2,1)} %collective-permute-done, ...), kind=kOutput, calls=%fused_computation.24 | convolution fusion | flops 851927040 | bytes 5603328 | tf_op jit(solution)/shard_map/dot_general | solution.py:65
  47.9 1.9 %select_convert_fusion.6 = bf16[18,34,256]{2,1,0:T(8,128)(2,1)S(1)} fusion(bf16[2,20,2,256]{3,2,1,0:T(2,128)(2,1)S(1)} %collective-permute-done.3, bf16[2,20,2,256]{3,2,1,0:T(2,128)(2,1)S(1)} %collective-permute-done.2, bf16[2,2,32,256]{3,2,1,0:T(8,128)(2,1)} %collective-permute-done.1, bf16[2,2,32,256]{3,2,1,0:T(8,128)(2,1)} %collective-permute-done, ...), kind=kOutput, calls=%fused_computation.25 | convolution fusion | flops 724137984 | bytes 5050368 | tf_op jit(solution)/shard_map/dot_general | solution.py:65
  50.6 0.8 select_bitcast_fusion.3
  51.6 0.8 copy.56
  52.5 1.0 select_convert_fusion.4
  53.6 6.5 %collective-permute-start.8 = (bf16[1,64,128]{2,1,0:T(8,128)(2,1)S(1)}, bf16[1,64,128]{2,1,0:T(8,128)(2,1)S(1)}, u32[]{:S(2)}, u32[]{:S(2)}) collective-permute-start(bf16[1,64,128]{2,1,0:T(8,128)(2,1)S(1)} %get-tuple-element.25), channel_id=1, source_target_pairs={{0,4},{4,8},{8,12},{12,16},{16,20},{20,24},{24,28},{1,5},{5,9},{9,... | collective-permute-start | bytes 49160 | tf_op jit(solution)/shard_map/ppermute | solution.py:17
  60.1 1.9 %collective-permute-start.9 = (bf16[1,64,128]{2,1,0:T(8,128)(2,1)S(1)}, bf16[1,64,128]{2,1,0:T(8,128)(2,1)S(1)}, u32[]{:S(2)}, u32[]{:S(2)}) collective-permute-start(bf16[1,64,128]{2,1,0:T(8,128)(2,1)S(1)} %get-tuple-element.26), channel_id=1, source_target_pairs={{4,0},{8,4},{12,8},{16,12},{20,16},{24,20},{28,24},{5,1},{9,5},{13... | collective-permute-start | bytes 49160 | tf_op jit(solution)/shard_map/ppermute | solution.py:19
  62.0 4.0 %collective-permute-done.9 = bf16[1,64,128]{2,1,0:T(8,128)(2,1)S(1)} collective-permute-done((bf16[1,64,128]{2,1,0:T(8,128)(2,1)S(1)}, bf16[1,64,128]{2,1,0:T(8,128)(2,1)S(1)}, u32[]{:S(2)}, u32[]{:S(2)}) %collective-permute-start.9) | collective-permute-done | bytes 16416 | tf_op jit(solution)/shard_map/ppermute | solution.py:19
  66.1 2.1 %collective-permute-start.10 = (bf16[34,1,128]{2,1,0:T(2,128)(2,1)S(1)}, bf16[34,1,128]{2,1,0:T(2,128)(2,1)S(1)}, u32[]{:S(2)}, u32[]{:S(2)}) collective-permute-start(bf16[34,1,128]{2,1,0:T(2,128)(2,1)S(1)} %get-tuple-element.14), channel_id=1, source_target_pairs={{1,0},{2,1},{3,2},{5,4},{6,5},{7,6},{9,8},{10,9},{11,10},{13,12},{... | collective-permute-start | bytes 26120 | tf_op jit(solution)/shard_map/ppermute | solution.py:19
  68.2 3.4 %collective-permute-start.11 = (bf16[34,1,128]{2,1,0:T(2,128)(2,1)S(1)}, bf16[34,1,128]{2,1,0:T(2,128)(2,1)S(1)}, u32[]{:S(2)}, u32[]{:S(2)}) collective-permute-start(bf16[34,1,128]{2,1,0:T(2,128)(2,1)S(1)} %get-tuple-element.13), channel_id=1, source_target_pairs={{0,1},{1,2},{2,3},{4,5},{5,6},{6,7},{8,9},{9,10},{10,11},{12,13},{... | collective-permute-start | bytes 26120 | tf_op jit(solution)/shard_map/ppermute | solution.py:17
  71.8 0.9 collective-permute-done.11
  74.4 1.4 %fusion.1 = bf16[32,64,128]{2,1,0:T(8,128)(2,1)S(1)} fusion(bf16[32,64,9,128]{3,1,2,0:T(8,128)(2,1)S(1)} %fusion.18, bf16[9,128,128,1]{1,2,0,3:T(8,128)(2,1)S(1)} %bitcast.329, bf16[32,64,128]{2,1,0:T(8,128)(2,1)S(1)} %copy-done.19), kind=kOutput, calls=%fused_computation.5 | convolution fusion | flops 604766208 | bytes 6062080 | tf_op jit(solution)/shard_map/dot_general | solution.py:65
  75.9 3.4 %collective-permute-start.12 = (bf16[1,64,128]{2,1,0:T(8,128)(2,1)S(1)}, bf16[1,64,128]{2,1,0:T(8,128)(2,1)S(1)}, u32[]{:S(2)}, u32[]{:S(2)}) collective-permute-start(bf16[1,64,128]{2,1,0:T(8,128)(2,1)S(1)} %get-tuple-element.23), channel_id=1, source_target_pairs={{0,4},{4,8},{8,12},{12,16},{16,20},{20,24},{24,28},{1,5},{5,9},{9,... | collective-permute-start | bytes 49160 | tf_op jit(solution)/shard_map/ppermute | solution.py:17
  79.2 1.9 %collective-permute-start.13 = (bf16[1,64,128]{2,1,0:T(8,128)(2,1)S(1)}, bf16[1,64,128]{2,1,0:T(8,128)(2,1)S(1)}, u32[]{:S(2)}, u32[]{:S(2)}) collective-permute-start(bf16[1,64,128]{2,1,0:T(8,128)(2,1)S(1)} %get-tuple-element.24), channel_id=1, source_target_pairs={{4,0},{8,4},{12,8},{16,12},{20,16},{24,20},{28,24},{5,1},{9,5},{13... | collective-permute-start | bytes 49160 | tf_op jit(solution)/shard_map/ppermute | solution.py:19
  81.2 4.0 %collective-permute-done.13 = bf16[1,64,128]{2,1,0:T(8,128)(2,1)S(1)} collective-permute-done((bf16[1,64,128]{2,1,0:T(8,128)(2,1)S(1)}, bf16[1,64,128]{2,1,0:T(8,128)(2,1)S(1)}, u32[]{:S(2)}, u32[]{:S(2)}) %collective-permute-start.13) | collective-permute-done | bytes 16416 | tf_op jit(solution)/shard_map/ppermute | solution.py:19
  85.2 1.9 %collective-permute-start.14 = (bf16[34,1,128]{2,1,0:T(2,128)(2,1)S(1)}, bf16[34,1,128]{2,1,0:T(2,128)(2,1)S(1)}, u32[]{:S(2)}, u32[]{:S(2)}) collective-permute-start(bf16[34,1,128]{2,1,0:T(2,128)(2,1)S(1)} %get-tuple-element.10), channel_id=1, source_target_pairs={{1,0},{2,1},{3,2},{5,4},{6,5},{7,6},{9,8},{10,9},{11,10},{13,12},{... | collective-permute-start | bytes 26120 | tf_op jit(solution)/shard_map/ppermute | solution.py:19
  87.2 3.4 %collective-permute-start.15 = (bf16[34,1,128]{2,1,0:T(2,128)(2,1)S(1)}, bf16[34,1,128]{2,1,0:T(2,128)(2,1)S(1)}, u32[]{:S(2)}, u32[]{:S(2)}) collective-permute-start(bf16[34,1,128]{2,1,0:T(2,128)(2,1)S(1)} %get-tuple-element.9), channel_id=1, source_target_pairs={{0,1},{1,2},{2,3},{4,5},{5,6},{6,7},{8,9},{9,10},{10,11},{12,13},{... | collective-permute-start | bytes 26120 | tf_op jit(solution)/shard_map/ppermute | solution.py:17
  90.8 0.7 eq.74
  91.5 0.7 eq.89
  92.2 0.7 eq.92
  92.9 0.7 eq.95
  95.1 1.8 %fusion.4 = (bf16[32,64,1,64]{3,1,0,2:T(8,128)(2,1)S(1)}, bf16[32,64,1,64]{3,1,0,2:T(8,128)(2,1)S(1)}, bf16[32,64,1,64]{3,1,0,2:T(8,128)(2,1)S(1)}, bf16[32,64,1,64]{3,1,0,2:T(8,128)(2,1)S(1)}) fusion(pred[32,64,64]{2,1,0:T(32,128)(4,1)S(1)} %eq.74, pred[32,64,64]{2,1,0:T(32,128)(4,1)S(1)} %eq.95, pred[32,64,64]{2,1,0:T(32,128)(4,1)S(1)} %eq.92, ...), kind=kOutput, calls=%fused_computation.30 | convolution fusion | flops 302514176 | bytes 6438912 | tf_op jit(solution)/shard_map/dot_general | solution.py:65
  97.9 2.2 %copy.68 = bf16[32,2,64,2,64]{4,3,2,1,0:T(2,128)(2,1)S(1)} copy(bf16[32,2,64,2,64]{4,2,0,3,1:T(8,128)(2,1)S(1)} %pad_maximum_fusion) | data formatting | bytes 2097152 | tf_op jit(solution)/shard_map/stack | solution.py:49
  100.1 2.5 %convert_element_type.41 = bf16[64,8192]{1,0:T(8,128)(2,1)} reshape(bf16[32,2,64,2,64]{4,3,2,1,0:T(2,128)(2,1)S(1)} %copy.68) | data formatting | bytes 2097152 | tf_op jit(solution)/shard_map/convert_element_type | solution.py:105
  (124 shorter events, 10.5 us)
Async XLA Ops:
  0.0 95.1 %copy-start = (bf16[128,576]{0,1:T(8,128)(2,1)S(1)}, bf16[128,576]{0,1:T(8,128)(2,1)}, u32[]{:S(2)}) copy-start(bf16[128,576]{0,1:T(8,128)(2,1)} %param.27) | copy-start | bytes 442372
  0.0 21.2 %copy-start.2 = (bf16[32,64,128]{2,1,0:T(8,128)(2,1)S(1)}, bf16[32,64,128]{2,1,0:T(8,128)(2,1)}, u32[]{:S(2)}) copy-start(bf16[32,64,128]{2,1,0:T(8,128)(2,1)} %param.21) | copy-start | bytes 1572868
  0.0 21.5 %copy-start.1 = (bf16[32,64,128]{2,1,0:T(8,128)(2,1)S(1)}, bf16[32,64,128]{2,1,0:T(8,128)(2,1)}, u32[]{:S(2)}) copy-start(bf16[32,64,128]{2,1,0:T(8,128)(2,1)} %param.17) | copy-start | bytes 1572868
  0.0 21.9 %copy-start.20 = (f32[128]{0:T(128)S(1)}, f32[128]{0:T(128)}, u32[]{:S(2)}) copy-start(f32[128]{0:T(128)} %param.25) | copy-start | bytes 1540
  0.0 23.6 %copy-start.3 = (bf16[256,2304]{1,0:T(8,128)(2,1)S(1)}, bf16[256,2304]{1,0:T(8,128)(2,1)}, u32[]{:S(2)}) copy-start(bf16[256,2304]{1,0:T(8,128)(2,1)} %param.31) | copy-start | bytes 3538948
  6.5 23.5 %collective-permute-start.4 = (bf16[3,32,256]{2,1,0:T(8,128)(2,1)}, bf16[3,32,256]{2,1,0:T(8,128)(2,1)}, u32[]{:S(2)}, u32[]{:S(2)}) collective-permute-start(bf16[3,32,256]{2,1,0:T(8,128)(2,1)} %get-tuple-element.39), channel_id=1, source_target_pairs={{0,4},{4,8},{8,12},{12,16},{16,20},{20,24},{24,28},{1,5},{5,9},{9,... | collective-permute-start | bytes 147464 | tf_op jit(solution)/shard_map/ppermute | solution.py:17
  10.2 19.8 %collective-permute-start.5 = (bf16[3,32,256]{2,1,0:T(8,128)(2,1)}, bf16[3,32,256]{2,1,0:T(8,128)(2,1)}, u32[]{:S(2)}, u32[]{:S(2)}) collective-permute-start(bf16[3,32,256]{2,1,0:T(8,128)(2,1)} %get-tuple-element.40), channel_id=1, source_target_pairs={{4,0},{8,4},{12,8},{16,12},{20,16},{24,20},{28,24},{5,1},{9,5},{13... | collective-permute-start | bytes 147464 | tf_op jit(solution)/shard_map/ppermute | solution.py:19
  13.6 22.5 %collective-permute-start = (bf16[2,2,32,256]{3,2,1,0:T(8,128)(2,1)}, bf16[2,2,32,256]{3,2,1,0:T(8,128)(2,1)}, u32[]{:S(2)}, u32[]{:S(2)}) collective-permute-start(bf16[2,2,32,256]{3,2,1,0:T(8,128)(2,1)} %get-tuple-element.27), channel_id=1, source_target_pairs={{0,4},{4,8},{8,12},{12,16},{16,20},{20,24},{24,28},{1,5},{5,9},{9,... | collective-permute-start | bytes 196616 | tf_op jit(solution)/shard_map/ppermute | solution.py:17
  18.2 18.0 %collective-permute-start.1 = (bf16[2,2,32,256]{3,2,1,0:T(8,128)(2,1)}, bf16[2,2,32,256]{3,2,1,0:T(8,128)(2,1)}, u32[]{:S(2)}, u32[]{:S(2)}) collective-permute-start(bf16[2,2,32,256]{3,2,1,0:T(8,128)(2,1)} %get-tuple-element.28), channel_id=1, source_target_pairs={{4,0},{8,4},{12,8},{16,12},{20,16},{24,20},{28,24},{5,1},{9,5},{13... | collective-permute-start | bytes 196616 | tf_op jit(solution)/shard_map/ppermute | solution.py:19
  21.9 6.1 %copy-start.17 = (f32[128]{0:T(128)}, f32[128]{0:T(128)S(1)}, u32[]{:S(2)}) copy-start(f32[128]{0:T(128)S(1)} %broadcast_multiply_fusion.3) | copy-start | bytes 1540
  21.9 6.1 %copy-start.12 = (f32[32,64]{1,0:T(8,128)}, f32[32,64]{1,0:T(8,128)S(1)}, u32[]{:S(2)}) copy-start(f32[32,64]{1,0:T(8,128)S(1)} %get-tuple-element.43) | copy-start | bytes 24580
  22.0 6.1 %copy-start.14 = (f32[32,64]{1,0:T(8,128)}, f32[32,64]{1,0:T(8,128)S(1)}, u32[]{:S(2)}) copy-start(f32[32,64]{1,0:T(8,128)S(1)} %get-tuple-element.44) | copy-start | bytes 24580
  23.6 12.5 %copy-start.5 = (bf16[16,32,256]{2,1,0:T(8,128)(2,1)S(1)}, bf16[16,32,256]{2,1,0:T(8,128)(2,1)}, u32[]{:S(2)}) copy-start(bf16[16,32,256]{2,1,0:T(8,128)(2,1)} %param.19) | copy-start | bytes 786436
  30.8 11.6 %collective-permute-start.6 = (bf16[22,3,256]{2,1,0:T(4,128)(2,1)S(1)}, bf16[22,3,256]{2,1,0:T(4,128)(2,1)S(1)}, u32[]{:S(2)}, u32[]{:S(2)}) collective-permute-start(bf16[22,3,256]{2,1,0:T(4,128)(2,1)S(1)} %get-tuple-element.29), channel_id=1, source_target_pairs={{0,1},{1,2},{2,3},{4,5},{5,6},{6,7},{8,9},{9,10},{10,11},{12,13},{... | collective-permute-start | bytes 101384 | tf_op jit(solution)/shard_map/ppermute | solution.py:17
  34.0 8.4 %collective-permute-start.7 = (bf16[22,3,256]{2,1,0:T(4,128)(2,1)S(1)}, bf16[22,3,256]{2,1,0:T(4,128)(2,1)S(1)}, u32[]{:S(2)}, u32[]{:S(2)}) collective-permute-start(bf16[22,3,256]{2,1,0:T(4,128)(2,1)S(1)} %get-tuple-element.30), channel_id=1, source_target_pairs={{1,0},{2,1},{3,2},{5,4},{6,5},{7,6},{9,8},{10,9},{11,10},{13,12},{... | collective-permute-start | bytes 101384 | tf_op jit(solution)/shard_map/ppermute | solution.py:19
  37.2 7.3 %collective-permute-start.2 = (bf16[2,20,2,256]{3,2,1,0:T(2,128)(2,1)S(1)}, bf16[2,20,2,256]{3,2,1,0:T(2,128)(2,1)S(1)}, u32[]{:S(2)}, u32[]{:S(2)}) collective-permute-start(bf16[2,20,2,256]{3,2,1,0:T(2,128)(2,1)S(1)} %get-tuple-element.5), channel_id=1, source_target_pairs={{0,1},{1,2},{2,3},{4,5},{5,6},{6,7},{8,9},{9,10},{10,11},{12,13},{... | collective-permute-start | bytes 122888 | tf_op jit(solution)/shard_map/ppermute | solution.py:17
  40.4 4.7 %collective-permute-start.3 = (bf16[2,20,2,256]{3,2,1,0:T(2,128)(2,1)S(1)}, bf16[2,20,2,256]{3,2,1,0:T(2,128)(2,1)S(1)}, u32[]{:S(2)}, u32[]{:S(2)}) collective-permute-start(bf16[2,20,2,256]{3,2,1,0:T(2,128)(2,1)S(1)} %get-tuple-element.6), channel_id=1, source_target_pairs={{1,0},{2,1},{3,2},{5,4},{6,5},{7,6},{9,8},{10,9},{11,10},{13,12},{... | collective-permute-start | bytes 122888 | tf_op jit(solution)/shard_map/ppermute | solution.py:19
  43.7 1.4 %copy-start.4 = (bf16[256,2304]{0,1:T(8,128)(2,1)S(1)}, bf16[256,2304]{0,1:T(8,128)(2,1)}, u32[]{:S(2)}) copy-start(bf16[256,2304]{0,1:T(8,128)(2,1)} %copy.48) | copy-start | bytes 3538948
  43.7 1.4 %copy-start.6 = (bf16[16,32,256]{2,1,0:T(8,128)(2,1)S(1)}, bf16[16,32,256]{2,1,0:T(8,128)(2,1)}, u32[]{:S(2)}) copy-start(bf16[16,32,256]{2,1,0:T(8,128)(2,1)} %param.18) | copy-start | bytes 786436
  49.7 0.8 copy-start.9
  49.8 0.9 copy-start.10
  49.8 0.9 copy-start.11
  51.4 1.1 %copy-start.13 = (f32[32,64]{1,0:T(8,128)S(1)}, f32[32,64]{1,0:T(8,128)}, u32[]{:S(2)}) copy-start(f32[32,64]{1,0:T(8,128)} %copy-done.12) | copy-start | bytes 24580
  51.4 1.1 %copy-start.15 = (f32[32,64]{1,0:T(8,128)S(1)}, f32[32,64]{1,0:T(8,128)}, u32[]{:S(2)}) copy-start(f32[32,64]{1,0:T(8,128)} %copy-done.14) | copy-start | bytes 24580
  51.4 1.1 %copy-start.16 = (f32[32,64]{1,0:T(8,128)S(1)}, f32[32,64]{1,0:T(8,128)}, u32[]{:S(2)}) copy-start(f32[32,64]{1,0:T(8,128)} %broadcast_multiply_fusion) | copy-start | bytes 24580
  51.5 1.1 %copy-start.18 = (f32[128]{0:T(128)S(1)}, f32[128]{0:T(128)}, u32[]{:S(2)}) copy-start(f32[128]{0:T(128)} %copy-done.17) | copy-start | bytes 1540
  51.6 20.0 %copy-start.8 = (bf16[128,1152]{1,0:T(8,128)(2,1)S(1)}, bf16[128,1152]{1,0:T(8,128)(2,1)}, u32[]{:S(2)}) copy-start(bf16[128,1152]{1,0:T(8,128)(2,1)} %param.28) | copy-start | bytes 884740
  53.6 8.5 %collective-permute-start.8 = (bf16[1,64,128]{2,1,0:T(8,128)(2,1)S(1)}, bf16[1,64,128]{2,1,0:T(8,128)(2,1)S(1)}, u32[]{:S(2)}, u32[]{:S(2)}) collective-permute-start(bf16[1,64,128]{2,1,0:T(8,128)(2,1)S(1)} %get-tuple-element.25), channel_id=1, source_target_pairs={{0,4},{4,8},{8,12},{12,16},{16,20},{20,24},{24,28},{1,5},{5,9},{9,... | collective-permute-start | bytes 49160 | tf_op jit(solution)/shard_map/ppermute | solution.py:17
  60.1 6.0 %collective-permute-start.9 = (bf16[1,64,128]{2,1,0:T(8,128)(2,1)S(1)}, bf16[1,64,128]{2,1,0:T(8,128)(2,1)S(1)}, u32[]{:S(2)}, u32[]{:S(2)}) collective-permute-start(bf16[1,64,128]{2,1,0:T(8,128)(2,1)S(1)} %get-tuple-element.26), channel_id=1, source_target_pairs={{4,0},{8,4},{12,8},{16,12},{20,16},{24,20},{28,24},{5,1},{9,5},{13... | collective-permute-start | bytes 49160 | tf_op jit(solution)/shard_map/ppermute | solution.py:19
  66.1 5.7 %collective-permute-start.10 = (bf16[34,1,128]{2,1,0:T(2,128)(2,1)S(1)}, bf16[34,1,128]{2,1,0:T(2,128)(2,1)S(1)}, u32[]{:S(2)}, u32[]{:S(2)}) collective-permute-start(bf16[34,1,128]{2,1,0:T(2,128)(2,1)S(1)} %get-tuple-element.14), channel_id=1, source_target_pairs={{1,0},{2,1},{3,2},{5,4},{6,5},{7,6},{9,8},{10,9},{11,10},{13,12},{... | collective-permute-start | bytes 26120 | tf_op jit(solution)/shard_map/ppermute | solution.py:19
  68.2 4.5 %collective-permute-start.11 = (bf16[34,1,128]{2,1,0:T(2,128)(2,1)S(1)}, bf16[34,1,128]{2,1,0:T(2,128)(2,1)S(1)}, u32[]{:S(2)}, u32[]{:S(2)}) collective-permute-start(bf16[34,1,128]{2,1,0:T(2,128)(2,1)S(1)} %get-tuple-element.13), channel_id=1, source_target_pairs={{0,1},{1,2},{2,3},{4,5},{5,6},{6,7},{8,9},{9,10},{10,11},{12,13},{... | collective-permute-start | bytes 26120 | tf_op jit(solution)/shard_map/ppermute | solution.py:17
  73.4 1.0 %copy-start.19 = (bf16[32,64,128]{2,1,0:T(8,128)(2,1)S(1)}, bf16[32,64,128]{2,1,0:T(8,128)(2,1)}, u32[]{:S(2)}) copy-start(bf16[32,64,128]{2,1,0:T(8,128)(2,1)} %param.16) | copy-start | bytes 1572868
  74.4 16.1 %copy-start.7 = (s32[32,4096]{1,0:T(8,128)S(1)}, s32[32,4096]{1,0:T(8,128)}, u32[]{:S(2)}) copy-start(s32[32,4096]{1,0:T(8,128)} %param.23) | copy-start | bytes 1572868
  75.9 5.3 %collective-permute-start.12 = (bf16[1,64,128]{2,1,0:T(8,128)(2,1)S(1)}, bf16[1,64,128]{2,1,0:T(8,128)(2,1)S(1)}, u32[]{:S(2)}, u32[]{:S(2)}) collective-permute-start(bf16[1,64,128]{2,1,0:T(8,128)(2,1)S(1)} %get-tuple-element.23), channel_id=1, source_target_pairs={{0,4},{4,8},{8,12},{12,16},{16,20},{20,24},{24,28},{1,5},{5,9},{9,... | collective-permute-start | bytes 49160 | tf_op jit(solution)/shard_map/ppermute | solution.py:17
  79.2 6.0 %collective-permute-start.13 = (bf16[1,64,128]{2,1,0:T(8,128)(2,1)S(1)}, bf16[1,64,128]{2,1,0:T(8,128)(2,1)S(1)}, u32[]{:S(2)}, u32[]{:S(2)}) collective-permute-start(bf16[1,64,128]{2,1,0:T(8,128)(2,1)S(1)} %get-tuple-element.24), channel_id=1, source_target_pairs={{4,0},{8,4},{12,8},{16,12},{20,16},{24,20},{28,24},{5,1},{9,5},{13... | collective-permute-start | bytes 49160 | tf_op jit(solution)/shard_map/ppermute | solution.py:19
  85.2 8.4 %collective-permute-start.14 = (bf16[34,1,128]{2,1,0:T(2,128)(2,1)S(1)}, bf16[34,1,128]{2,1,0:T(2,128)(2,1)S(1)}, u32[]{:S(2)}, u32[]{:S(2)}) collective-permute-start(bf16[34,1,128]{2,1,0:T(2,128)(2,1)S(1)} %get-tuple-element.10), channel_id=1, source_target_pairs={{1,0},{2,1},{3,2},{5,4},{6,5},{7,6},{9,8},{10,9},{11,10},{13,12},{... | collective-permute-start | bytes 26120 | tf_op jit(solution)/shard_map/ppermute | solution.py:19
  87.2 6.5 %collective-permute-start.15 = (bf16[34,1,128]{2,1,0:T(2,128)(2,1)S(1)}, bf16[34,1,128]{2,1,0:T(2,128)(2,1)S(1)}, u32[]{:S(2)}, u32[]{:S(2)}) collective-permute-start(bf16[34,1,128]{2,1,0:T(2,128)(2,1)S(1)} %get-tuple-element.9), channel_id=1, source_target_pairs={{0,1},{1,2},{2,3},{4,5},{5,6},{6,7},{8,9},{9,10},{10,11},{12,13},{... | collective-permute-start | bytes 26120 | tf_op jit(solution)/shard_map/ppermute | solution.py:17
where the time goes:
time: 104 us; the launch traced here: 103 us
  starting transfers between devices  47.1 us (45%)
  local copies, waits for them, and re-layouts  19.9 us (19%)
  other arithmetic  17.1 us (16%)
  waiting for transfers between devices  9.58 us (9%)
  matrix products  7.82 us (8%)
    ppermute x8, starting transfers between devices, extended(): lax.ppermute(tail, axis, [(i, (i + 1) % count) for i in range(ends)])  31.3 us
    ppermute x8, starting transfers between devices, extended(): lax.ppermute(head, axis, [((i + 1) % count, i) for i in range(ends)])  15.8 us
    unnamed x86, local copies, waits for them, and re-layouts  10.8 us
    ppermute x8, waiting for transfers between devices, extended(): lax.ppermute(head, axis, [((i + 1) % count, i) for i in range(ends)])  8.7 us
    dot_general x5, matrix products, back_conv(): result = jnp.dot(patches, arranged, preferred_element_type=jnp.float32)  7.82 us
    slice x3, other arithmetic, extended(): lax.slice_in_dim(cells, cells.shape[dim] - width, cells.shape[dim], axis=...  3.28 us
    another operation x2, local copies, waits for them, and re-layouts, unpool(): return jnp.stack(stripes, axis=1).reshape(2 * height, 2 * breadth, channels)  3 us
    eq x4, local copies, waits for them, and re-layouts, unpool(): position == 2 * vertical + lateral  2.77 us
  transfers between devices with their start and end apart: 16, of which 4 were waited for; matrix products, arithmetic and copies ran while one was open for 18% of the time, Pallas kernels for 0%

commit v1 on v0

v1 whole, which is shorter than its diff:
```python
import functools

import jax
import jax.numpy as jnp
from jax import lax
from jax.experimental import pallas as pl
from jax.experimental.pallas import tpu as pltpu
from jax.sharding import PartitionSpec as P

EPSILON = 1e-06
MESH = pl.DeviceIdType.MESH
F32 = jnp.float32
BF16 = jnp.bfloat16
SIDE = 8
OFF3 = 6
OFF2 = 4
OFFU = 2
DIRS = ((-1, 0), (1, 0), (0, -1), (0, 1), (-1, -1), (-1, 1), (1, -1), (1, 1))
HALOS = (4, 4, 3, 2, 2, 2, 1)


def message_shape(shape, halo, d):
    dr, dc = d
    return (halo if dr else shape[0], SIDE if dc else shape[1], shape[2])


def source_slices(shape, halo, d):
    dr, dc = d
    rows = slice(0, shape[0]) if dr == 0 else (slice(0, halo) if dr < 0 else slice(shape[0] - halo, shape[0]))
    cols = slice(0, shape[1]) if dc == 0 else (slice(0, SIDE) if dc < 0 else slice(shape[1] - SIDE, shape[1]))
    return rows, cols


def landing_slices(shape, halo, off, d):
    dr, dc = d
    first, count = {0: (0, shape[0]), -1: (shape[0], halo), 1: (-halo, halo)}[dr]
    if dc == 0:
        cols = slice(0, shape[1])
    elif dc < 0:
        cols = slice(shape[1], shape[1] + SIDE)
    else:
        cols = slice(shape[1] + SIDE, shape[1] + 2 * SIDE)
        first -= 1
    return slice(off + first, off + first + count), cols


def place(axes):
    return tuple(lax.axis_index(a) for a in axes)


def reachable(axes, counts, d, sign):
    checks = []
    for axis, count, step in zip(axes, counts, d):
        if step:
            target = lax.axis_index(axis) + sign * step
            checks.append(target >= 0 if sign * step < 0 else target < count)
    ok = checks[0]
    for c in checks[1:]:
        ok = jnp.logical_and(ok, c)
    return ok


def exchange_kernel(axes, counts, shapes, *refs):
    n = len(shapes)
    inputs, pool = refs[:n], refs[n]
    outs = refs[n + 1 : n + 1 + 8 * n]
    pool_outs = refs[n + 1 + 8 * n : n + 1 + 8 * n + 8]
    edge, edge_rows, local_sem, send_sem, recv_sem = refs[n + 1 + 8 * n + 8 :]
    depth = pool.shape[0]
    width = pool.shape[1] // 128
    top = pltpu.make_async_copy(pool.at[pl.ds(0, 8)], edge.at[0], local_sem.at[0])
    low = pltpu.make_async_copy(pool.at[pl.ds(depth - 8, 8)], edge.at[1], local_sem.at[1])
    top.start()
    low.start()
    barrier = pltpu.get_barrier_semaphore()
    me = place(axes)
    for d in DIRS:
        @pl.when(reachable(axes, counts, d, 1))
        def _():
            pl.semaphore_signal(barrier, inc=1, device_id=(me[0] + d[0], me[1] + d[1]), device_id_type=MESH)
    spans = [1 + jnp.minimum(m, 1) + jnp.minimum(c - 1 - m, 1) for m, c in zip(me, counts)]
    pl.semaphore_wait(barrier, spans[0] * spans[1] - 1)

    def copy(a, k):
        d = DIRS[k]
        if a < n:
            rows, cols = source_slices(shapes[a], HALOS[a], d)
            src, dst = inputs[a].at[rows, cols], outs[8 * a + k]
        else:
            dst = pool_outs[k]
            if d[1] == 0:
                src = edge_rows.at[0 if d[0] < 0 else 1]
            else:
                rows = {0: slice(0, depth), -1: slice(0, 8), 1: slice(depth - 8, depth)}[d[0]]
                lanes = slice(0, 128) if d[1] < 0 else slice((width - 1) * 128, width * 128)
                src = pool.at[rows, lanes]
        return pltpu.make_async_remote_copy(
            src_ref=src, dst_ref=dst, send_sem=send_sem.at[a, k], recv_sem=recv_sem.at[a, k],
            device_id=(me[0] + d[0], me[1] + d[1]), device_id_type=MESH)

    for a in range(n):
        for k in range(8):
            @pl.when(reachable(axes, counts, DIRS[k], 1))
            def _():
                copy(a, k).start()
    top.wait()
    low.wait()
    for j in range(width):
        edge_rows[0, j : j + 1, :] = edge[0, 0:1, j * 128 : (j + 1) * 128]
        edge_rows[1, j : j + 1, :] = edge[1, 7:8, j * 128 : (j + 1) * 128]
    for k in range(8):
        @pl.when(reachable(axes, counts, DIRS[k], 1))
        def _():
            copy(n, k).start()
    for a in range(n + 1):
        for k in range(8):
            @pl.when(reachable(axes, counts, DIRS[k], 1))
            def _():
                copy(a, k).wait_send()

            @pl.when(reachable(axes, counts, DIRS[k], -1))
            def _():
                copy(a, k).wait_recv()


def injected(p, t, weight):
    f = jnp.maximum(p, 0.0)
    g = jnp.maximum(t, 0.0)
    rinv = lax.rsqrt(jnp.mean(f * f, axis=-1, keepdims=True) + EPSILON)
    sinv = lax.rsqrt(jnp.mean(g * g, axis=-1, keepdims=True) + EPSILON)
    u = f * rinv
    e = weight * (u - g * sinv)
    return (e - u * jnp.mean(e * u, axis=-1, keepdims=True)) * rinv


def shifted_sum(z, n):
    length = z.shape[0]
    return pltpu.roll(z[:, :n], length - 1, 0) + z[:, n : 2 * n] + pltpu.roll(z[:, 2 * n :], 1, 0)


def conv_rows(x, w, first, rows, stride, n):
    length = rows * stride + 32
    start = first * stride - 16
    parts = [x[pl.ds(pl.multiple_of(start + (1 - dy) * stride, 16), length), :] for dy in range(3)]
    z = jnp.dot(jnp.concatenate(parts, axis=1), w[...], preferred_element_type=F32)
    return shifted_sum(z, n)[16 : 16 + rows * stride]


def body_kernel(axes, counts, shapes, *refs):
    n = len(shapes)
    inputs = refs[:n]
    pool1, pool2, lin2, lin3, k21, k22, k31, k32, k33 = refs[n : n + 9]
    halos = refs[n + 9 : n + 9 + 8 * n]
    pool_halos = refs[n + 9 + 8 * n : n + 17 + 8 * n]
    out = refs[n + 17 + 8 * n]
    scratch = refs[n + 18 + 8 * n :]
    bufs = scratch[:n]
    (x33, x32, x31, x22, x21, w33, w32, w31, w22, w21, k21v, p1, p2, prow, pcol, pcor, upy, upp, yt, tmp, res,
     in_sem, halo_sem, w_sem, pool_sem, ph_sem, out_sem) = scratch[n:]
    off = [OFF3, OFF3, OFF3, OFF3, OFF2, OFF2, OFF2]
    h3, wd3 = shapes[0][0], shapes[0][1]
    h2, wd2 = shapes[4][0], shapes[4][1]
    s3, s2 = wd3 + 2 * SIDE, wd2 + 2 * SIDE

    def own(a):
        return pltpu.make_async_copy(
            inputs[a], bufs[a].at[off[a] : off[a] + shapes[a][0], 0 : shapes[a][1]], in_sem.at[a])

    def halo(a, k):
        rows, cols = landing_slices(shapes[a], HALOS[a], off[a], DIRS[k])
        return pltpu.make_async_copy(halos[8 * a + k], bufs[a].at[rows, cols], halo_sem.at[a, k])

    def weights(i):
        k, w = ((k33, w33), (k32, w32), (k31, w31), (k22, w22))[i]
        o, cols = k.shape[0], k.shape[1] // 3
        return [pltpu.make_async_copy(k.at[:, dy * cols : (dy + 1) * cols], w.at[dy * o : (dy + 1) * o], w_sem.at[i, dy])
                for dy in range(3)]

    def pool_halo(k):
        dr, dc = DIRS[k]
        dst = prow.at[k] if dc == 0 else (pcol.at[k - 2] if dr == 0 else pcor.at[k - 4])
        return pltpu.make_async_copy(pool_halos[k], dst, ph_sem.at[k])

    others = (pltpu.make_async_copy(k21, k21v, pool_sem.at[0]), pltpu.make_async_copy(pool1, p1, pool_sem.at[1]),
              pltpu.make_async_copy(pool2, p2, pool_sem.at[2]))

    def arrive(a, act):
        act(own(a))
        for k in range(8):
            @pl.when(reachable(axes, counts, DIRS[k], -1))
            def _():
                act(halo(a, k))

    start, wait = (lambda c: c.start()), (lambda c: c.wait())
    arrive(0, start)
    arrive(1, start)
    for c in weights(0):
        c.start()
    arrive(2, start)
    for c in weights(1):
        c.start()
    arrive(3, start)
    for c in weights(2):
        c.start()
    for c in others:
        c.start()
    for k in range(8):
        pool_halo(k).start()
    for a in (4, 5, 6):
        arrive(a, start)
    for c in weights(3):
        c.start()
    for a in (0, 2, 3, 4, 6):
        for k in range(8):
            @pl.when(jnp.logical_not(reachable(axes, counts, DIRS[k], -1)))
            def _():
                rows, cols = landing_slices(shapes[a], HALOS[a], off[a], DIRS[k])
                dst = bufs[a].at[rows, cols]
                dst[...] = jnp.zeros(dst.shape, BF16)

    arrive(0, wait)
    arrive(1, wait)
    c3 = shapes[0][2]
    c2 = shapes[4][2]
    weight3 = 2.0 * lin3[...]
    weight2 = 2.0 * lin2[...]

    @pl.loop(0, bufs[0].shape[0] // 2)
    def _(i):
        p = bufs[0][pl.ds(2 * i, 2)].reshape(2 * s3, c3).astype(F32)
        t = bufs[1][pl.ds(2 * i, 2)].reshape(2 * s3, c3).astype(F32)
        seed = jnp.where(p > 0, injected(p, t, weight3), 0.0).astype(BF16)
        x33[pl.ds(pl.multiple_of(2 * i * s3, 16), 2 * s3), :] = seed

    def masked_conv(x, w, p, y, first, rows, steps, stride, channels):
        @pl.loop(0, steps)
        def _(i):
            at = first + i * rows
            o = conv_rows(x, w, at, rows, stride, channels)
            pre = p[pl.ds(at, rows)].reshape(rows * stride, channels).astype(F32)
            y[pl.ds(pl.multiple_of(at * stride, 16), rows * stride), :] = jnp.where(pre > 0, o, 0.0).astype(BF16)

    arrive(2, wait)
    for c in weights(0):
        c.wait()
    masked_conv(x33, w33, bufs[2], x32, OFF3 - 4, (h3 + 8) // 3, 3, s3, c3)
    arrive(3, wait)
    for c in weights(1):
        c.wait()
    masked_conv(x32, w32, bufs[3], x31, OFF3 - 3, (h3 + 5) // 3, 3, s3, c3)

    for c in others:
        c.wait()
    for k in range(8):
        pool_halo(k).wait()
    for j in range(wd3):
        for i0 in range(0, h3, 8):
            blk = p2[i0 : i0 + 8, j * 128 : (j + 1) * 128]
            for b in range(2):
                upp[pl.ds((OFFU + i0) * s2 + 2 * j + b, 8, stride=s2), :] = blk
    for b in range(2):
        upp[pl.ds((OFFU + h3) * s2 + b, wd3, stride=2), :] = prow[0]
        upp[pl.ds((OFFU - 1) * s2 + b, wd3, stride=2), :] = prow[1]
        for i0 in range(0, h3, 8):
            upp[pl.ds((OFFU + i0) * s2 + wd2 + b, 8, stride=s2), :] = pcol[0, i0 : i0 + 8]
            upp[pl.ds((OFFU + i0) * s2 + s2 - 2 + b, 8, stride=s2), :] = pcol[1, i0 : i0 + 8]
        upp[(OFFU + h3) * s2 + wd2 + b : (OFFU + h3) * s2 + wd2 + b + 1, :] = pcor[0, 0:1]
        upp[(OFFU + h3) * s2 + s2 - 2 + b : (OFFU + h3) * s2 + s2 - 2 + b + 1, :] = pcor[1, 0:1]
        upp[(OFFU - 1) * s2 + wd2 + b : (OFFU - 1) * s2 + wd2 + b + 1, :] = pcor[2, 7:8]
        upp[(OFFU - 1) * s2 + s2 - 2 + b : (OFFU - 1) * s2 + s2 - 2 + b + 1, :] = pcor[3, 7:8]

    for c in weights(2):
        c.wait()
    rows31 = (h3 + 4) // 4

    @pl.loop(0, 4)
    def _(i):
        o = conv_rows(x31, w31, OFF3 - 2 + i * rows31, rows31, s3, c2)
        for q in range(rows31):
            row = i * rows31 + q
            base = row * s2
            y = o[q * s3 : (q + 1) * s3]
            for b in range(2):
                upy[pl.ds(base + b, wd3, stride=2), :] = y[:wd3]
                upy[pl.ds(base + wd2 + b, 4, stride=2), :] = y[wd3 : wd3 + 4]
                upy[pl.ds(base + s2 + s2 - 8 + b, 4, stride=2), :] = y[s3 - 4 :]

    arrive(4, wait)
    arrive(5, wait)
    main = s2 - 8
    par = lax.broadcasted_iota(jnp.int32, (s2, 128), 0) % 2

    @pl.loop(0, h2 + 5)
    def _(i):
        for_row = i + OFF2 - 3
        r0 = (i + 1) // 2 + OFFU - 2
        a0 = (i + 1) % 2
        r1 = (i + 2) // 2 + OFFU - 2
        a1 = (i + 2) % 2
        at0 = pl.multiple_of(r0 * s2, 8)
        at1 = pl.multiple_of(r1 * s2 + main, 8)
        y = jnp.concatenate([upy[pl.ds(at0, main), :], upy[pl.ds(at1, 8), :]], axis=0)
        m = jnp.concatenate([upp[pl.ds(at0, main), :] - 2 * a0, upp[pl.ds(at1, 8), :] - 2 * a1], axis=0)
        p = bufs[4][for_row].astype(F32)
        t = bufs[5][for_row].astype(F32)
        arriving = jnp.where(m == par, y, 0.0) + injected(p, t, weight2)
        x22[pl.ds(pl.multiple_of(for_row * s2, 16), s2), :] = jnp.where(p > 0, arriving, 0.0).astype(BF16)

    arrive(6, wait)
    for c in weights(3):
        c.wait()
    masked_conv(x22, w22, bufs[6], x21, OFF2 - 2, (h2 + 3) // 5, 5, s2, c2)

    low_half = lax.broadcasted_iota(jnp.int32, (c2, 128), 1) < 64
    for tap in range(9):
        dy, dx = tap // 3, tap % 3
        width = min(128, 576 - (tap // 2) * 128)
        blk = k21v[:, (tap // 2) * 128 : (tap // 2) * 128 + width].astype(F32)
        if width < 128:
            blk = jnp.concatenate([blk, blk], axis=1)
        else:
            turned = pltpu.roll(blk, 64, 1)
            blk = jnp.where(low_half, blk, turned) if tap % 2 == 0 else jnp.where(low_half, turned, blk)
        w21[dy * c2 : (dy + 1) * c2, dx * 128 : (dx + 1) * 128] = blk.astype(BF16)

    rows21 = 8

    @pl.loop(0, h2 // rows21)
    def _(i):
        o = conv_rows(x21, w21, OFF2 + i * rows21, rows21, s2, 128)
        for q in range(rows21):
            for j0 in range(0, wd2, 8):
                y = o[q * s2 + j0 : q * s2 + j0 + 8]
                for a in range(2):
                    yt[pl.ds(j0 * 2 * h2 + 2 * (i * rows21 + q) + a, 8, stride=2 * h2), :] = y

    lane_low = lax.broadcasted_iota(jnp.int32, (2 * h2, 128), 1) < 64
    want = (lax.broadcasted_iota(jnp.int32, (2 * h2, 128), 0) % 2) * 2 + jnp.where(lane_low, 0, 1)

    @pl.loop(0, wd2 // 2)
    def _(g):
        lanes = pl.ds(pl.multiple_of(g * 128, 128), 128)
        blk = p1[:, lanes]
        for a in range(2):
            tmp[pl.ds(a, h2, stride=2), :] = blk
        m = tmp[...]
        turned = pltpu.roll(m, 64, 1)
        for e in range(2):
            y = yt[pl.ds(pl.multiple_of((2 * g + e) * 2 * h2, 8), 2 * h2), :]
            sel = jnp.where(lane_low, m, turned) if e == 0 else jnp.where(lane_low, turned, m)
            res[:, pl.ds(pl.multiple_of((2 * g + e) * 128, 128), 128)] = jnp.where(sel == want, y, 0.0).astype(BF16)

    done = pltpu.make_async_copy(res, out, out_sem)
    done.start()
    done.wait()


def shards(axes, counts, relu21, relu22, relu31, relu32, relu33, target22, target33, pool1, pool2, lin2, lin3,
           k21, k22, k31, k32, k33):
    tensors = (relu33, target33, relu32, relu31, relu22, target22, relu21)
    shapes = tuple(t.shape for t in tensors)
    n = len(tensors)
    h3, wd3, c3 = relu33.shape
    h2, wd2, c2 = relu22.shape
    s3, s2 = wd3 + 2 * SIDE, wd2 + 2 * SIDE
    anywhere = pl.BlockSpec(memory_space=pl.ANY)
    vmem = pl.BlockSpec(memory_space=pltpu.VMEM)
    halo_shapes = [jax.ShapeDtypeStruct(message_shape(s, h, d), BF16) for s, h in zip(shapes, HALOS) for d in DIRS]
    for d in DIRS:
        shape = (wd3, 128) if d[1] == 0 else ((h3, 128) if d[0] == 0 else (8, 128))
        halo_shapes.append(jax.ShapeDtypeStruct(shape, jnp.int32))
    halos = pl.pallas_call(
        functools.partial(exchange_kernel, axes, counts, shapes),
        out_shape=halo_shapes,
        in_specs=[anywhere] * (n + 1),
        out_specs=[anywhere] * len(halo_shapes),
        scratch_shapes=[
            pltpu.VMEM((2, 8, pool2.shape[1]), jnp.int32),
            pltpu.VMEM((2, wd3, 128), jnp.int32),
            pltpu.SemaphoreType.DMA((2,)),
            pltpu.SemaphoreType.DMA((n + 1, 8)),
            pltpu.SemaphoreType.DMA((n + 1, 8)),
        ],
        compiler_params=pltpu.CompilerParams(collective_id=0, has_side_effects=True),
        name="exchange",
    )(*tensors, pool2)
    rows3, rows2 = h3 + 2 * OFF3, h2 + 2 * OFF2
    scratch = [pltpu.VMEM((rows3, s3, c3), BF16)] * 4 + [pltpu.VMEM((rows2, s2, c2), BF16)] * 3
    scratch += [pltpu.VMEM((rows3 * s3, c3), BF16)] * 3 + [pltpu.VMEM((rows2 * s2, c2), BF16)] * 2
    scratch += [pltpu.VMEM((3 * k.shape[0], k.shape[1] // 3), BF16) for k in (k33, k32, k31, k22)]
    scratch += [
        pltpu.VMEM((3 * c2, 384), BF16),
        pltpu.VMEM(k21.shape, BF16),
        pltpu.VMEM(pool1.shape, jnp.int32),
        pltpu.VMEM(pool2.shape, jnp.int32),
        pltpu.VMEM((2, wd3, 128), jnp.int32),
        pltpu.VMEM((2, h3, 128), jnp.int32),
        pltpu.VMEM((4, 8, 128), jnp.int32),
        pltpu.VMEM(((h3 + 2 * OFFU + 1) * s2, 128), F32),
        pltpu.VMEM(((h3 + 2 * OFFU + 1) * s2, 128), jnp.int32),
        pltpu.VMEM((wd2 * 2 * h2, 128), F32),
        pltpu.VMEM((2 * h2, 128), jnp.int32),
        pltpu.VMEM((2 * h2, wd2 * 128), BF16),
        pltpu.SemaphoreType.DMA((n,)),
        pltpu.SemaphoreType.DMA((n, 8)),
        pltpu.SemaphoreType.DMA((4, 3)),
        pltpu.SemaphoreType.DMA((3,)),
        pltpu.SemaphoreType.DMA((8,)),
        pltpu.SemaphoreType.DMA(()),
    ]
    return pl.pallas_call(
        functools.partial(body_kernel, axes, counts, shapes),
        out_shape=jax.ShapeDtypeStruct((2 * h2, wd2 * 128), BF16),
        in_specs=[anywhere] * (n + 2) + [vmem] * 2 + [anywhere] * (5 + len(halo_shapes)),
        out_specs=anywhere,
        scratch_shapes=scratch,
        compiler_params=pltpu.CompilerParams(vmem_limit_bytes=56 * 1024 * 1024),
        name="body",
    )(*tensors, pool1, pool2, lin2.reshape(1, c2), lin3.reshape(1, c3), k21, k22, k31, k32, k33, *halos)


def solution(mesh):
    axes = ("row", "col")
    counts = tuple(mesh.shape[a] for a in axes)
    cells = P("row", "col", None)
    in_specs = (cells,) * 7 + (P("row", "col"),) * 2 + (P(),) * 7
    return jax.shard_map(functools.partial(shards, axes, counts), mesh=mesh, in_specs=in_specs,
                         out_specs=P("row", "col"), check_vma=False)
```

time: 104 us -> 50.1 us (0.48); the launches traced: 103 us -> 49.9 us
  Pallas kernels: 0 us -> 48.2 us
  starting transfers between devices: 47.1 us -> 0 us
  local copies, waits for them, and re-layouts: 19.9 us -> 1.71 us
  other arithmetic: 17.1 us -> 0 us
  waiting for transfers between devices: 9.58 us -> 0 us
  matrix products: 7.82 us -> 0 us
    pallas_call x0 -> x2, Pallas kernels: none -> 48.2 us  [the longest x1 27.9 us: shards(): pl.pallas_call(functools.partial(body_kernel, axes, counts, shapes), out_...]
    ppermute x16 -> x0, starting transfers between devices: 47.1 us -> none  [the longest x8 31.3 us: extended(): lax.ppermute(tail, axis, [(i, (i + 1) % count) for i in range(ends)])]
    ppermute x16 -> x0, waiting for transfers between devices: 9.58 us -> none  [the longest x8 8.7 us: extended(): lax.ppermute(head, axis, [((i + 1) % count, i) for i in range(ends)])]
    unnamed x86 -> x1, local copies, waits for them, and re-layouts: 10.8 us -> 1.71 us
    dot_general x5 -> x0, matrix products: 7.82 us -> none  [back_conv(): result = jnp.dot(patches, arranged, preferred_element_type=jnp.float32)]
    reduce_sum x6 -> x0, other arithmetic: 5.45 us -> none  [the longest x2 2.42 us: inject(): jnp.mean(excess * scaled, axis=-1, keepdims=True)]
    slice x3 -> x0, other arithmetic: 3.28 us -> none  [extended(): lax.slice_in_dim(cells, cells.shape[dim] - width, cells.shape[dim], axis=...]
    another operation x7 -> x0, local copies, waits for them, and re-layouts: 3.27 us -> none  [the longest x2 3 us: unpool(): return jnp.stack(stripes, axis=1).reshape(2 * height, 2 * breadth, channels)]
  transfers between devices with their start and end apart: 16 -> 0, of which waited for: 4 -> 0; matrix products, arithmetic and copies ran while one was open for 18% -> 0% of each run, Pallas kernels for 0% -> 0%
where the time goes in v1:
time: 50.1 us; the launch traced here: 49.9 us
  Pallas kernels  48.2 us (96%)
  local copies, waits for them, and re-layouts  1.71 us (3%)
    pallas_call x1, Pallas kernels, shards(): pl.pallas_call(functools.partial(body_kernel, axes, counts, shapes), out_...  27.9 us
    pallas_call x1, Pallas kernels, shards(): pl.pallas_call(functools.partial(exchange_kernel, axes, counts, shapes),...  20.2 us
    unnamed x1, local copies, waits for them, and re-layouts  1.71 us

profile of v1, /device:TPU:11, one launch (start us, length us, event | category | flops | bytes accessed | tf_op | source)
XLA Modules:
  0.0 49.9 jit_solution(7370584865177806866)
XLA Ops:
  0.0 1.7 %copy.17.refs_11_ = bf16[128,576]{1,0:T(8,128)(2,1)} copy(bf16[128,576]{0,1:T(8,128)(2,1)} %param.27) | data formatting | bytes 294912 | tf_op args[11]
  1.7 20.2 %exchange.1 = (bf16[4,32,256]{2,1,0:T(8,128)(2,1)}, bf16[4,32,256]{2,1,0:T(8,128)(2,1)}, bf16[16,8,256]{2,1,0:T(8,128)(2,1)}, bf16[16,8,256]{2,1,0:T(8,128)(2,1)...) custom-call(bf16[16,32,256]{2,1,0:T(8,128)(2,1)} %refs_0_.3, ...), custom_call_target="tpu_custom_call" | custom-call | tf_op jit(solution)/shard_map/exchange/pallas_call | solution.py:372
  21.9 27.9 %body.1 = bf16[64,8192]{1,0:T(8,128)(2,1)} custom-call(bf16[16,32,256]{2,1,0:T(8,128)(2,1)} %refs_0_.3, bf16[16,32,256]{2,1,0:T(8,128)(2,1)} %refs_1_.3, bf16[16,32,256]{2,1,0:T(8,128)(2,1)} %refs_2_.3, bf16[16,32,256]{2,1,0:T(8,128)(2,1)} %refs_3_.3, bf16[32,64,128]{2,1,0:T(8,128)(2,1)} %refs_4_.3, bf16[32,64,128]{2,1,0:T(8,128)(2,1)} %refs_5_.3, ...), custom_call_target="tpu_custom_call" | custom-call | tf_op jit(solution)/shard_map/body/pallas_call | solution.py:411

commit v2 on v1

v2 whole, which is shorter than its diff:
```python
import functools

import jax
import jax.numpy as jnp
from jax import lax
from jax.experimental import pallas as pl
from jax.experimental.pallas import tpu as pltpu
from jax.sharding import PartitionSpec as P

EPSILON = 1e-06
MESH = pl.DeviceIdType.MESH
F32 = jnp.float32
BF16 = jnp.bfloat16
SIDE = 8
OFF3 = 6
OFF2 = 4
OFFU = 2
DIRS = ((-1, 0), (1, 0), (0, -1), (0, 1), (-1, -1), (-1, 1), (1, -1), (1, 1))


WIDTHS = (4, 4, 2, 2, 2, 1)
ROWS = (4, 3, 2, 2, 2, 1)


def reachable(axes, counts, d, sign):
    checks = []
    for axis, count, step in zip(axes, counts, d):
        if step:
            target = lax.axis_index(axis) + sign * step
            checks.append(target >= 0 if sign * step < 0 else target < count)
    ok = checks[0]
    for c in checks[1:]:
        ok = jnp.logical_and(ok, c)
    return ok


def packed(tiles, width, side):
    k = SIDE // width
    rows, _, c = tiles.shape
    grouped = tiles.reshape(rows // k, k, SIDE, c)
    sub = lax.broadcasted_iota(jnp.int32, (rows // k, SIDE, c), 1)
    total = None
    for i in range(k):
        shift = (i * width - (0 if side == 0 else SIDE - width)) % SIDE
        piece = grouped[:, i]
        if shift:
            piece = pltpu.roll(piece, shift, 1)
        total = piece if total is None else jnp.where(sub >= i * width, piece, total)
    return total


def unpacked(tiles, width, side):
    k = SIDE // width
    count, _, c = tiles.shape
    pieces = []
    for i in range(k):
        shift = ((0 if side == 0 else SIDE - width) - i * width) % SIDE
        pieces.append(pltpu.roll(tiles, shift, 1) if shift else tiles)
    return jnp.stack(pieces, axis=1).reshape(count * k, SIDE, c)


def injected(p, t, weight):
    f = jnp.maximum(p, 0.0)
    g = jnp.maximum(t, 0.0)
    rinv = lax.rsqrt(jnp.mean(f * f, axis=-1, keepdims=True) + EPSILON)
    sinv = lax.rsqrt(jnp.mean(g * g, axis=-1, keepdims=True) + EPSILON)
    u = f * rinv
    e = weight * (u - g * sinv)
    return (e - u * jnp.mean(e * u, axis=-1, keepdims=True)) * rinv


def shifted_sum(z, n):
    length = z.shape[0]
    return pltpu.roll(z[:, :n], length - 1, 0) + z[:, n : 2 * n] + pltpu.roll(z[:, 2 * n :], 1, 0)


def conv_rows(x, w, first, rows, stride, n):
    length = rows * stride + 32
    start = first * stride - 16
    parts = [x[pl.ds(pl.multiple_of(start + (1 - dy) * stride, 16), length), :] for dy in range(3)]
    z = jnp.dot(jnp.concatenate(parts, axis=1), w[...], preferred_element_type=F32)
    return shifted_sum(z, n)[16 : 16 + rows * stride]


def body_kernel(axes, counts, shapes, *refs):
    (relu33, target33, relu32, relu31, relu22, target22, relu21,
     pool1, pool2, lin2, lin3, k21, k22, k31, k32, k33, out) = refs[:17]
    scratch = refs[17:]
    inputs = (None, relu32, relu31, relu22, target22, relu21)
    p33, t33 = scratch[:2]
    bufs = (None,) + tuple(scratch[2:7])
    sides, side_in, corner_in = scratch[7:13], scratch[13:19], scratch[19:25]
    (x33, x32, x31, x22, x21, w33, w32, w31, w22, w21, k21v, p1, p2, pedge, prow, pcol, pcor, upy, upp, yt, tmp, res,
     own_sem, w_sem, misc_sem, seed_send, seed_recv, send_sem, recv_sem, out_sem) = scratch[25:]
    n = 6
    off = [OFF3, OFF3, OFF3, OFF2, OFF2, OFF2]
    h3, wd3, c3 = shapes[0]
    h2, wd2, c2 = shapes[3]
    s3, s2 = wd3 + 2 * SIDE, wd2 + 2 * SIDE

    def own(a):
        return pltpu.make_async_copy(
            inputs[a], bufs[a].at[off[a] : off[a] + shapes[a][0], 0 : shapes[a][1]], own_sem.at[a])

    def weights(i):
        k, w = ((k33, w33), (k32, w32), (k31, w31), (k22, w22))[i]
        o, cols = k.shape[0], k.shape[1] // 3
        return [pltpu.make_async_copy(k.at[:, dy * cols : (dy + 1) * cols], w.at[dy * o : (dy + 1) * o], w_sem.at[i, dy])
                for dy in range(3)]

    others = [pltpu.make_async_copy(src, dst, misc_sem.at[i])
              for i, (src, dst) in enumerate(((relu33, p33), (target33, t33), (pool2, p2), (pool1, p1), (k21, k21v)))]
    others[0].start()
    others[1].start()
    for a in (1, 2, 3, 4, 5):
        own(a).start()
    others[2].start()
    for i in range(4):
        for c in weights(i):
            c.start()
    others[4].start()
    others[3].start()

    me = tuple(lax.axis_index(axis) for axis in axes)

    def peer(d):
        return (me[0] + d[0], me[1] + d[1])

    barrier = pltpu.get_barrier_semaphore()
    for d in DIRS:
        @pl.when(reachable(axes, counts, d, 1))
        def _():
            pl.semaphore_signal(barrier, inc=1, device_id=peer(d), device_id_type=MESH)
    spans = [1 + jnp.minimum(m, 1) + jnp.minimum(c - 1 - m, 1) for m, c in zip(me, counts)]
    pl.semaphore_wait(barrier, spans[0] * spans[1] - 1)

    def remote(src, dst, ssem, rsem, d):
        return pltpu.make_async_remote_copy(
            src_ref=src, dst_ref=dst, send_sem=ssem, recv_sem=rsem, device_id=peer(d), device_id_type=MESH)

    def corner_tiles(a):
        k = SIDE // WIDTHS[a]
        return -(-ROWS[a] // k)

    def messages(a, k):
        d = DIRS[k]
        ssem, rsem = send_sem.at[a, k], recv_sem.at[a, k]
        if a == n:
            if d[1] == 0:
                return [remote(pedge.at[k], prow.at[k], ssem, rsem, d)]
            rows = {0: slice(0, h3), -1: slice(0, 8), 1: slice(h3 - 8, h3)}[d[0]]
            lanes = slice(0, 128) if d[1] < 0 else slice((wd3 - 1) * 128, wd3 * 128)
            dst = pcol.at[k - 2] if d[0] == 0 else pcor.at[k - 4]
            return [remote(pool2.at[rows, lanes], dst, ssem, rsem, d)]
        if d[1] == 0:
            h, rows = ROWS[a], shapes[a][0]
            first, land = (0, rows) if d[0] < 0 else (rows - h, -h)
            if a == 0:
                return [remote(x33.at[(OFF3 + first + q) * s3 : (OFF3 + first + q) * s3 + wd3],
                               x33.at[(OFF3 + land + q) * s3 : (OFF3 + land + q) * s3 + wd3],
                               seed_send.at[k, q], seed_recv.at[k, q], d) for q in range(h)]
            return [remote(inputs[a].at[first : first + h],
                           bufs[a].at[off[a] + land : off[a] + land + h, 0 : shapes[a][1]], ssem, rsem, d)]
        side = 0 if d[1] < 0 else 1
        if d[0] == 0:
            return [remote(sides[a].at[side], side_in[a].at[side], ssem, rsem, d)]
        tiles, total = corner_tiles(a), sides[a].shape[1]
        first = 0 if d[0] < 0 else total - tiles
        return [remote(sides[a].at[side, first : first + tiles], corner_in[a].at[k - 4], ssem, rsem, d)]

    def send(a, ks):
        for k in ks:
            @pl.when(reachable(axes, counts, DIRS[k], 1))
            def _():
                for c in messages(a, k):
                    c.start()

    def put(a, row, slot, tiles):
        count = tiles.shape[0]
        tiles = tiles.astype(BF16)
        if a == 0:
            for q in range(count):
                at = (OFF3 + row + q) * s3 + slot
                x33[at : at + SIDE, :] = tiles[q]
        else:
            bufs[a][off[a] + row : off[a] + row + count, slot : slot + SIDE, :] = tiles

    def receive(a):
        h, (rows, cols, c) = ROWS[a], shapes[a]
        for k in range(8):
            d = DIRS[k]
            first, count = {0: (0, rows), -1: (rows, h), 1: (-h, h)}[d[0]]
            side = 0 if d[1] < 0 else 1
            slot = cols if side == 0 else cols + SIDE

            @pl.when(reachable(axes, counts, d, -1))
            def _():
                for m in messages(a, k):
                    m.wait_recv()
                if d[1]:
                    tiles = side_in[a][side] if d[0] == 0 else corner_in[a][k - 4]
                    spread = unpacked(tiles.astype(F32), WIDTHS[a], side)
                    spread = spread[:count] if d[0] <= 0 else spread[spread.shape[0] - count :]
                    put(a, first - side, slot, spread)

            if a != 4:
                @pl.when(jnp.logical_not(reachable(axes, counts, d, -1)))
                def _():
                    if d[1]:
                        put(a, first - side, slot, jnp.zeros((count, SIDE, c), F32))
                    elif a == 0:
                        for q in range(count):
                            x33[(OFF3 + first + q) * s3 : (OFF3 + first + q) * s3 + wd3, :] = jnp.zeros((wd3, c), BF16)
                    else:
                        bufs[a][off[a] + first : off[a] + first + count, 0:cols, :] = jnp.zeros((count, cols, c), BF16)

    def pack(a, side):
        rows, cols, c = shapes[a]
        at = 0 if side == 0 else cols - SIDE
        if a == 0:
            tiles = jnp.stack([x33[(OFF3 + q) * s3 + at : (OFF3 + q) * s3 + at + SIDE, :] for q in range(rows)])
        else:
            tiles = bufs[a][off[a] : off[a] + rows, at : at + SIDE, :]
        sides[a][side] = packed(tiles.astype(F32), WIDTHS[a], side).astype(BF16)

    weight3 = 2.0 * lin3[...]
    weight2 = 2.0 * lin2[...]
    others[0].wait()
    others[1].wait()

    @pl.loop(0, h3 // 2)
    def _(i):
        for q in range(2):
            p = p33[2 * i + q].astype(F32)
            t = t33[2 * i + q].astype(F32)
            seed = jnp.where(p > 0, injected(p, t, weight3), 0.0).astype(BF16)
            x33[pl.ds(pl.multiple_of((OFF3 + 2 * i + q) * s3, 16), wd3), :] = seed

    send(0, (0, 1))
    pack(0, 0)
    pack(0, 1)
    send(0, range(2, 8))
    for a in (1, 2, 3, 4, 5):
        send(a, (0, 1))
        own(a).wait()
        pack(a, 0)
        pack(a, 1)
        send(a, range(2, 8))
        if a == 2:
            others[2].wait()
            for j in range(wd3):
                pedge[0, j : j + 1, :] = p2[0:1, j * 128 : (j + 1) * 128]
                pedge[1, j : j + 1, :] = p2[h3 - 1 : h3, j * 128 : (j + 1) * 128]
            send(n, range(8))

    def masked_conv(x, w, p, y, first, rows, steps, stride, channels):
        @pl.loop(0, steps)
        def _(i):
            at = first + i * rows
            o = conv_rows(x, w, at, rows, stride, channels)
            pre = p[pl.ds(at, rows)].reshape(rows * stride, channels).astype(F32)
            y[pl.ds(pl.multiple_of(at * stride, 16), rows * stride), :] = jnp.where(pre > 0, o, 0.0).astype(BF16)

    for j in range(wd3):
        for i0 in range(0, h3, 8):
            blk = p2[i0 : i0 + 8, j * 128 : (j + 1) * 128]
            for b in range(2):
                upp[pl.ds((OFFU + i0) * s2 + 2 * j + b, 8, stride=s2), :] = blk
    others[4].wait()
    for tap in range(9):
        dy, dx = tap // 3, tap % 3
        rows = k21v[tap * 64 : (tap + 1) * 64, :].astype(F32)
        w21[dy * c2 : (dy + 1) * c2, dx * 128 : (dx + 1) * 128] = jnp.concatenate([rows, rows], axis=0).T.astype(BF16)
    receive(0)
    for c in weights(0):
        c.wait()
    receive(1)
    masked_conv(x33, w33, bufs[1], x32, OFF3 - 4, (h3 + 8) // 3, 3, s3, c3)
    receive(2)
    for c in weights(1):
        c.wait()
    masked_conv(x32, w32, bufs[2], x31, OFF3 - 3, (h3 + 5) // 3, 3, s3, c3)

    for k in range(8):
        @pl.when(reachable(axes, counts, DIRS[k], -1))
        def _():
            for m in messages(n, k):
                m.wait_recv()
    for b in range(2):
        upp[pl.ds((OFFU + h3) * s2 + b, wd3, stride=2), :] = prow[0]
        upp[pl.ds((OFFU - 1) * s2 + b, wd3, stride=2), :] = prow[1]
        for i0 in range(0, h3, 8):
            upp[pl.ds((OFFU + i0) * s2 + wd2 + b, 8, stride=s2), :] = pcol[0, i0 : i0 + 8]
            upp[pl.ds((OFFU + i0) * s2 + s2 - 2 + b, 8, stride=s2), :] = pcol[1, i0 : i0 + 8]
        upp[(OFFU + h3) * s2 + wd2 + b : (OFFU + h3) * s2 + wd2 + b + 1, :] = pcor[0, 0:1]
        upp[(OFFU + h3) * s2 + s2 - 2 + b : (OFFU + h3) * s2 + s2 - 2 + b + 1, :] = pcor[1, 0:1]
        upp[(OFFU - 1) * s2 + wd2 + b : (OFFU - 1) * s2 + wd2 + b + 1, :] = pcor[2, 7:8]
        upp[(OFFU - 1) * s2 + s2 - 2 + b : (OFFU - 1) * s2 + s2 - 2 + b + 1, :] = pcor[3, 7:8]

    for c in weights(2):
        c.wait()
    rows31 = (h3 + 4) // 4

    @pl.loop(0, 4)
    def _(i):
        o = conv_rows(x31, w31, OFF3 - 2 + i * rows31, rows31, s3, c2)
        for q in range(rows31):
            row = i * rows31 + q
            base = row * s2
            y = o[q * s3 : (q + 1) * s3]
            for b in range(2):
                upy[pl.ds(base + b, wd3, stride=2), :] = y[:wd3]
                upy[pl.ds(base + wd2 + b, 4, stride=2), :] = y[wd3 : wd3 + 4]
                upy[pl.ds(base + s2 + s2 - 8 + b, 4, stride=2), :] = y[s3 - 4 :]

    receive(3)
    receive(4)
    main = s2 - 8
    par = lax.broadcasted_iota(jnp.int32, (s2, 128), 0) % 2

    @pl.loop(0, h2 + 5)
    def _(i):
        for_row = i + OFF2 - 3
        r0 = (i + 1) // 2 + OFFU - 2
        a0 = (i + 1) % 2
        r1 = (i + 2) // 2 + OFFU - 2
        a1 = (i + 2) % 2
        at0 = pl.multiple_of(r0 * s2, 8)
        at1 = pl.multiple_of(r1 * s2 + main, 8)
        y = jnp.concatenate([upy[pl.ds(at0, main), :], upy[pl.ds(at1, 8), :]], axis=0)
        m = jnp.concatenate([upp[pl.ds(at0, main), :] - 2 * a0, upp[pl.ds(at1, 8), :] - 2 * a1], axis=0)
        p = bufs[3][for_row].astype(F32)
        t = bufs[4][for_row].astype(F32)
        arriving = jnp.where(m == par, y, 0.0) + injected(p, t, weight2)
        x22[pl.ds(pl.multiple_of(for_row * s2, 16), s2), :] = jnp.where(p > 0, arriving, 0.0).astype(BF16)

    receive(5)
    for c in weights(3):
        c.wait()
    masked_conv(x22, w22, bufs[5], x21, OFF2 - 2, (h2 + 3) // 5, 5, s2, c2)

    rows21 = 8

    @pl.loop(0, h2 // rows21)
    def _(i):
        o = conv_rows(x21, w21, OFF2 + i * rows21, rows21, s2, 128)
        for q in range(rows21):
            for j0 in range(0, wd2, 8):
                y = o[q * s2 + j0 : q * s2 + j0 + 8]
                for a in range(2):
                    yt[pl.ds(j0 * 2 * h2 + 2 * (i * rows21 + q) + a, 8, stride=2 * h2), :] = y

    others[3].wait()
    lane_low = lax.broadcasted_iota(jnp.int32, (2 * h2, 128), 1) < 64
    want = (lax.broadcasted_iota(jnp.int32, (2 * h2, 128), 0) % 2) * 2 + jnp.where(lane_low, 0, 1)

    @pl.loop(0, wd2 // 2)
    def _(g):
        lanes = pl.ds(pl.multiple_of(g * 128, 128), 128)
        blk = p1[:, lanes]
        for a in range(2):
            tmp[pl.ds(a, h2, stride=2), :] = blk
        m = tmp[...]
        turned = pltpu.roll(m, 64, 1)
        for e in range(2):
            y = yt[pl.ds(pl.multiple_of((2 * g + e) * 2 * h2, 8), 2 * h2), :]
            sel = jnp.where(lane_low, m, turned) if e == 0 else jnp.where(lane_low, turned, m)
            res[:, pl.ds(pl.multiple_of((2 * g + e) * 128, 128), 128)] = jnp.where(sel == want, y, 0.0).astype(BF16)

    done = pltpu.make_async_copy(res, out, out_sem)
    done.start()
    for a in range(n + 1):
        for k in range(8):
            @pl.when(reachable(axes, counts, DIRS[k], 1))
            def _():
                for m in messages(a, k):
                    m.wait_send()
    done.wait()


def shards(axes, counts, relu21, relu22, relu31, relu32, relu33, target22, target33, pool1, pool2, lin2, lin3,
           k21, k22, k31, k32, k33):
    tensors = (relu33, target33, relu32, relu31, relu22, target22, relu21)
    shapes = tuple(t.shape for t in (relu33, relu32, relu31, relu22, target22, relu21))
    h3, wd3, c3 = relu33.shape
    h2, wd2, c2 = relu22.shape
    s3, s2 = wd3 + 2 * SIDE, wd2 + 2 * SIDE
    anywhere = pl.BlockSpec(memory_space=pl.ANY)
    vmem = pl.BlockSpec(memory_space=pltpu.VMEM)
    rows3, rows2 = h3 + 2 * OFF3, h2 + 2 * OFF2
    per = [SIDE // w for w in WIDTHS]
    scratch = [pltpu.VMEM((h3, wd3, c3), BF16)] * 2
    scratch += [pltpu.VMEM((rows3, s3, c3), BF16)] * 2 + [pltpu.VMEM((rows2, s2, c2), BF16)] * 3
    scratch += [pltpu.VMEM((2, s[0] // k, SIDE, s[2]), BF16) for s, k in zip(shapes, per)] * 2
    scratch += [pltpu.VMEM((4, -(-r // k), SIDE, s[2]), BF16) for s, k, r in zip(shapes, per, ROWS)]
    scratch += [pltpu.VMEM((rows3 * s3, c3), BF16)] * 3 + [pltpu.VMEM((rows2 * s2, c2), BF16)] * 2
    scratch += [pltpu.VMEM((3 * k.shape[0], k.shape[1] // 3), BF16) for k in (k33, k32, k31, k22)]
    scratch += [
        pltpu.VMEM((3 * c2, 384), BF16),
        pltpu.VMEM(k21.shape[::-1], BF16),
        pltpu.VMEM(pool1.shape, jnp.int32),
        pltpu.VMEM(pool2.shape, jnp.int32),
        pltpu.VMEM((2, wd3, 128), jnp.int32),
        pltpu.VMEM((2, wd3, 128), jnp.int32),
        pltpu.VMEM((2, h3, 128), jnp.int32),
        pltpu.VMEM((4, 8, 128), jnp.int32),
        pltpu.VMEM(((h3 + 2 * OFFU + 1) * s2, 128), F32),
        pltpu.VMEM(((h3 + 2 * OFFU + 1) * s2, 128), jnp.int32),
        pltpu.VMEM((wd2 * 2 * h2, 128), F32),
        pltpu.VMEM((2 * h2, 128), jnp.int32),
        pltpu.VMEM((2 * h2, wd2 * 128), BF16),
        pltpu.SemaphoreType.DMA((6,)),
        pltpu.SemaphoreType.DMA((4, 3)),
        pltpu.SemaphoreType.DMA((5,)),
        pltpu.SemaphoreType.DMA((2, 4)),
        pltpu.SemaphoreType.DMA((2, 4)),
        pltpu.SemaphoreType.DMA((7, 8)),
        pltpu.SemaphoreType.DMA((7, 8)),
        pltpu.SemaphoreType.DMA(()),
    ]
    return pl.pallas_call(
        functools.partial(body_kernel, axes, counts, shapes),
        out_shape=jax.ShapeDtypeStruct((2 * h2, wd2 * 128), BF16),
        in_specs=[anywhere] * 9 + [vmem] * 2 + [anywhere] * 5,
        out_specs=anywhere,
        scratch_shapes=scratch,
        compiler_params=pltpu.CompilerParams(
            vmem_limit_bytes=56 * 1024 * 1024, collective_id=0, has_side_effects=True),
        name="body",
    )(*tensors, pool1, pool2, lin2.reshape(1, c2), lin3.reshape(1, c3), k21.T, k22, k31, k32, k33)


def solution(mesh):
    axes = ("row", "col")
    counts = tuple(mesh.shape[a] for a in axes)
    cells = P("row", "col", None)
    in_specs = (cells,) * 7 + (P("row", "col"),) * 2 + (P(),) * 7
    return jax.shard_map(functools.partial(shards, axes, counts), mesh=mesh, in_specs=in_specs,
                         out_specs=P("row", "col"), check_vma=False)
```

time: 50.1 us -> 36.8 us (0.73)
  Pallas kernels: 48.2 us -> 34.1 us
  local copies, waits for them, and re-layouts: 1.71 us -> 2.26 us
    pallas_call x1 -> x0, Pallas kernels: 20.2 us -> none  [shards(): pl.pallas_call(functools.partial(exchange_kernel, axes, counts, shapes),...]
    pallas_call x1, Pallas kernels: 27.9 us -> 34.1 us  [shards(): pl.pallas_call(functools.partial(body_kernel, axes, counts, shapes), out_...]
    unnamed x1, local copies, waits for them, and re-layouts: 1.71 us -> 2.26 us
where the time goes in v2:
time: 36.8 us; the launch traced here: 36.4 us
  Pallas kernels  34.1 us (93%)
  local copies, waits for them, and re-layouts  2.26 us (6%)
    pallas_call x1, Pallas kernels, shards(): pl.pallas_call(functools.partial(body_kernel, axes, counts, shapes), out_...  34.1 us
    unnamed x1, local copies, waits for them, and re-layouts  2.26 us

profile of v2, /device:TPU:11, one launch (start us, length us, event | category | flops | bytes accessed | tf_op | source)
XLA Modules:
  0.0 36.4 jit_solution(5758105859249817171)
XLA Ops:
  0.0 34.1 %body.1 = bf16[64,8192]{1,0:T(8,128)(2,1)} custom-call(bf16[16,32,256]{2,1,0:T(8,128)(2,1)} %refs_0_.1, bf16[16,32,256]{2,1,0:T(8,128)(2,1)} %refs_1_.1, bf16[16,32,256]{2,1,0:T(8,128)(2,1)} %refs_2_.1, bf16[16,32,256]{2,1,0:T(8,128)(2,1)} %refs_3_.1, bf16[32,64,128]{2,1,0:T(8,128)(2,1)} %refs_4_.1, bf16[32,64,128]{2,1,0:T(8,128)(2,1)} %refs_5_.1, ...), custom_call_target="tpu_custom_call" | custom-call | tf_op jit(solution)/shard_map/body/pallas_call | solution.py:421
  34.1 2.3 %copy.18 = bf16[64,8192]{1,0:T(8,128)(2,1)} copy(bf16[64,8192]{1,0:T(8,128)(2,1)} %body.1) | data formatting | bytes 2097152

commit v3 on v2

--- a/solution.py
+++ b/solution.py
@@ -90,7 +90,7 @@
     p33, t33 = scratch[:2]
     bufs = (None,) + tuple(scratch[2:7])
     sides, side_in, corner_in = scratch[7:13], scratch[13:19], scratch[19:25]
-    (x33, x32, x31, x22, x21, w33, w32, w31, w22, w21, k21v, p1, p2, pedge, prow, pcol, pcor, upy, upp, yt, tmp, res,
+    (x33, x32, x31, x22, x21, w33, w32, w31, w22, w21, k21v, p1, p2, pedge, prow, pcol, pcor, upy, upp, yt, twice, injs, res,
      own_sem, w_sem, misc_sem, seed_send, seed_recv, send_sem, recv_sem, out_sem) = scratch[25:]
     n = 6
     off = [OFF3, OFF3, OFF3, OFF2, OFF2, OFF2]
@@ -271,6 +271,27 @@
         dy, dx = tap // 3, tap % 3
         rows = k21v[tap * 64 : (tap + 1) * 64, :].astype(F32)
         w21[dy * c2 : (dy + 1) * c2, dx * 128 : (dx + 1) * 128] = jnp.concatenate([rows, rows], axis=0).T.astype(BF16)
+    rows2 = bufs[3].shape[0]
+
+    def inject_at(row, count, slot, width):
+        p = bufs[3][pl.ds(row, count), slot : slot + width, :].reshape(count * width, c2).astype(F32)
+        t = bufs[4][pl.ds(row, count), slot : slot + width, :].reshape(count * width, c2).astype(F32)
+        value = injected(p, t, weight2)
+        for q in range(count):
+            injs[pl.ds(pl.multiple_of((row + q) * s2 + slot, 16), width), :] = value[q * width : (q + 1) * width]
+
+    @pl.loop(0, h2 // 4)
+    def _(i):
+        inject_at(OFF2 + 4 * i, 4, 0, wd2)
+
+    others[3].wait()
+
+    @pl.loop(0, wd2 // 2)
+    def _(g):
+        blk = p1[:, pl.ds(pl.multiple_of(g * 128, 128), 128)]
+        for a in range(2):
+            twice[pl.ds(g * 2 * h2 + a, h2, stride=2), :] = blk
+
     receive(0)
     for c in weights(0):
         c.wait()
@@ -315,24 +336,29 @@
 
     receive(3)
     receive(4)
+    for q in range(0, rows2, SIDE):
+        inject_at(q, SIDE, wd2, 2 * SIDE)
+    inject_at(OFF2 - 2, 2, 0, wd2)
+    inject_at(OFF2 + h2, 2, 0, wd2)
     main = s2 - 8
     par = lax.broadcasted_iota(jnp.int32, (s2, 128), 0) % 2
 
-    @pl.loop(0, h2 + 5)
-    def _(i):
-        for_row = i + OFF2 - 3
-        r0 = (i + 1) // 2 + OFFU - 2
-        a0 = (i + 1) % 2
-        r1 = (i + 2) // 2 + OFFU - 2
-        a1 = (i + 2) % 2
-        at0 = pl.multiple_of(r0 * s2, 8)
-        at1 = pl.multiple_of(r1 * s2 + main, 8)
-        y = jnp.concatenate([upy[pl.ds(at0, main), :], upy[pl.ds(at1, 8), :]], axis=0)
-        m = jnp.concatenate([upp[pl.ds(at0, main), :] - 2 * a0, upp[pl.ds(at1, 8), :] - 2 * a1], axis=0)
-        p = bufs[3][for_row].astype(F32)
-        t = bufs[4][for_row].astype(F32)
-        arriving = jnp.where(m == par, y, 0.0) + injected(p, t, weight2)
-        x22[pl.ds(pl.multiple_of(for_row * s2, 16), s2), :] = jnp.where(p > 0, arriving, 0.0).astype(BF16)
+    @pl.loop(0, (h2 + 6) // 2)
+    def _(half):
+        for i in (2 * half, 2 * half + 1):
+            for_row = i + OFF2 - 3
+            r0 = (i + 1) // 2 + OFFU - 2
+            a0 = (i + 1) % 2
+            r1 = (i + 2) // 2 + OFFU - 2
+            a1 = (i + 2) % 2
+            at0 = pl.multiple_of(r0 * s2, 8)
+            at1 = pl.multiple_of(r1 * s2 + main, 8)
+            here = pl.ds(pl.multiple_of(for_row * s2, 16), s2)
+            y = jnp.concatenate([upy[pl.ds(at0, main), :], upy[pl.ds(at1, 8), :]], axis=0)
+            m = jnp.concatenate([upp[pl.ds(at0, main), :] - 2 * a0, upp[pl.ds(at1, 8), :] - 2 * a1], axis=0)
+            p = bufs[3][for_row].astype(F32)
+            arriving = jnp.where(m == par, y, 0.0) + injs[here, :]
+            x22[here, :] = jnp.where(p > 0, arriving, 0.0).astype(BF16)
 
     receive(5)
     for c in weights(3):
@@ -350,32 +376,32 @@
                 for a in range(2):
                     yt[pl.ds(j0 * 2 * h2 + 2 * (i * rows21 + q) + a, 8, stride=2 * h2), :] = y
 
-    others[3].wait()
     lane_low = lax.broadcasted_iota(jnp.int32, (2 * h2, 128), 1) < 64
     want = (lax.broadcasted_iota(jnp.int32, (2 * h2, 128), 0) % 2) * 2 + jnp.where(lane_low, 0, 1)
-
-    @pl.loop(0, wd2 // 2)
-    def _(g):
-        lanes = pl.ds(pl.multiple_of(g * 128, 128), 128)
-        blk = p1[:, lanes]
-        for a in range(2):
-            tmp[pl.ds(a, h2, stride=2), :] = blk
-        m = tmp[...]
-        turned = pltpu.roll(m, 64, 1)
-        for e in range(2):
-            y = yt[pl.ds(pl.multiple_of((2 * g + e) * 2 * h2, 8), 2 * h2), :]
-            sel = jnp.where(lane_low, m, turned) if e == 0 else jnp.where(lane_low, turned, m)
-            res[:, pl.ds(pl.multiple_of((2 * g + e) * 128, 128), 128)] = jnp.where(sel == want, y, 0.0).astype(BF16)
-
-    done = pltpu.make_async_copy(res, out, out_sem)
-    done.start()
+    share = wd2 // 8
+    parts = []
+    for part in range(4):
+        @pl.loop(0, share)
+        def _(v):
+            g = part * share + v
+            m = twice[pl.ds(pl.multiple_of(g * 2 * h2, 8), 2 * h2), :]
+            turned = pltpu.roll(m, 64, 1)
+            for e in range(2):
+                y = yt[pl.ds(pl.multiple_of((2 * g + e) * 2 * h2, 8), 2 * h2), :]
+                sel = jnp.where(lane_low, m, turned) if e == 0 else jnp.where(lane_low, turned, m)
+                res[:, pl.ds(pl.multiple_of((2 * g + e) * 128, 128), 128)] = jnp.where(sel == want, y, 0.0).astype(BF16)
+
+        lanes = slice(part * share * 256, (part + 1) * share * 256)
+        parts.append(pltpu.make_async_copy(res.at[:, lanes], out.at[:, lanes], out_sem.at[part]))
+        parts[-1].start()
     for a in range(n + 1):
         for k in range(8):
             @pl.when(reachable(axes, counts, DIRS[k], 1))
             def _():
                 for m in messages(a, k):
                     m.wait_send()
-    done.wait()
+    for c in parts:
+        c.wait()
 
 
 def shards(axes, counts, relu21, relu22, relu31, relu32, relu33, target22, target33, pool1, pool2, lin2, lin3,
@@ -407,7 +433,8 @@
         pltpu.VMEM(((h3 + 2 * OFFU + 1) * s2, 128), F32),
         pltpu.VMEM(((h3 + 2 * OFFU + 1) * s2, 128), jnp.int32),
         pltpu.VMEM((wd2 * 2 * h2, 128), F32),
-        pltpu.VMEM((2 * h2, 128), jnp.int32),
+        pltpu.VMEM((wd2 * h2, 128), jnp.int32),
+        pltpu.VMEM((rows2 * s2, c2), F32),
         pltpu.VMEM((2 * h2, wd2 * 128), BF16),
         pltpu.SemaphoreType.DMA((6,)),
         pltpu.SemaphoreType.DMA((4, 3)),
@@ -416,7 +443,7 @@
         pltpu.SemaphoreType.DMA((2, 4)),
         pltpu.SemaphoreType.DMA((7, 8)),
         pltpu.SemaphoreType.DMA((7, 8)),
-        pltpu.SemaphoreType.DMA(()),
+        pltpu.SemaphoreType.DMA((4,)),
     ]
     return pl.pallas_call(
         functools.partial(body_kernel, axes, counts, shapes),

time: 36.8 us -> 30.5 us (0.83)
  Pallas kernels: 34.1 us -> 27.8 us
    pallas_call x1, Pallas kernels: 34.1 us -> 27.8 us  [shards(): pl.pallas_call(functools.partial(body_kernel, axes, counts, shapes), out_...]
where the time goes in v3:
time: 30.5 us; the launch traced here: 30.1 us
  Pallas kernels  27.8 us (91%)
  local copies, waits for them, and re-layouts  2.26 us (7%)
    pallas_call x1, Pallas kernels, shards(): pl.pallas_call(functools.partial(body_kernel, axes, counts, shapes), out_...  27.8 us
    unnamed x1, local copies, waits for them, and re-layouts  2.26 us

profile of v3, /device:TPU:11, one launch (start us, length us, event | category | flops | bytes accessed | tf_op | source)
XLA Modules:
  0.0 30.1 jit_solution(2691323227060131749)
XLA Ops:
  0.0 27.8 %body.1 = bf16[64,8192]{1,0:T(8,128)(2,1)} custom-call(bf16[16,32,256]{2,1,0:T(8,128)(2,1)} %refs_0_.1, bf16[16,32,256]{2,1,0:T(8,128)(2,1)} %refs_1_.1, bf16[16,32,256]{2,1,0:T(8,128)(2,1)} %refs_2_.1, bf16[16,32,256]{2,1,0:T(8,128)(2,1)} %refs_3_.1, bf16[32,64,128]{2,1,0:T(8,128)(2,1)} %refs_4_.1, bf16[32,64,128]{2,1,0:T(8,128)(2,1)} %refs_5_.1, ...), custom_call_target="tpu_custom_call" | custom-call | tf_op jit(solution)/shard_map/body/pallas_call | solution.py:448
  27.8 2.3 %copy.18 = bf16[64,8192]{1,0:T(8,128)(2,1)} copy(bf16[64,8192]{1,0:T(8,128)(2,1)} %body.1) | data formatting | bytes 2097152

commit v4 on v3

--- a/solution.py
+++ b/solution.py
@@ -225,33 +225,40 @@
 
     weight3 = 2.0 * lin3[...]
     weight2 = 2.0 * lin2[...]
-    others[0].wait()
-    others[1].wait()
-
-    @pl.loop(0, h3 // 2)
-    def _(i):
+    def send_all(a):
+        send(a, (0, 1))
+        own(a).wait()
+        pack(a, 0)
+        pack(a, 1)
+        send(a, range(2, 8))
+
+    def seed_rows(i):
         for q in range(2):
             p = p33[2 * i + q].astype(F32)
             t = t33[2 * i + q].astype(F32)
             seed = jnp.where(p > 0, injected(p, t, weight3), 0.0).astype(BF16)
             x33[pl.ds(pl.multiple_of((OFF3 + 2 * i + q) * s3, 16), wd3), :] = seed
 
+    send_all(1)
+    others[0].wait()
+    others[1].wait()
+    outer = ROWS[0] // 2
+
+    @pl.loop(0, outer)
+    def _(i):
+        seed_rows(i)
+        seed_rows(h3 // 2 - outer + i)
+
     send(0, (0, 1))
+
+    @pl.loop(outer, h3 // 2 - outer)
+    def _(i):
+        seed_rows(i)
+
     pack(0, 0)
     pack(0, 1)
     send(0, range(2, 8))
-    for a in (1, 2, 3, 4, 5):
-        send(a, (0, 1))
-        own(a).wait()
-        pack(a, 0)
-        pack(a, 1)
-        send(a, range(2, 8))
-        if a == 2:
-            others[2].wait()
-            for j in range(wd3):
-                pedge[0, j : j + 1, :] = p2[0:1, j * 128 : (j + 1) * 128]
-                pedge[1, j : j + 1, :] = p2[h3 - 1 : h3, j * 128 : (j + 1) * 128]
-            send(n, range(8))
+    send_all(2)
 
     def masked_conv(x, w, p, y, first, rows, steps, stride, channels):
         @pl.loop(0, steps)
@@ -260,6 +267,13 @@
             o = conv_rows(x, w, at, rows, stride, channels)
             pre = p[pl.ds(at, rows)].reshape(rows * stride, channels).astype(F32)
             y[pl.ds(pl.multiple_of(at * stride, 16), rows * stride), :] = jnp.where(pre > 0, o, 0.0).astype(BF16)
+
+    others[2].wait()
+    for j in range(wd3):
+        pedge[0, j : j + 1, :] = p2[0:1, j * 128 : (j + 1) * 128]
+        pedge[1, j : j + 1, :] = p2[h3 - 1 : h3, j * 128 : (j + 1) * 128]
+    for a in (3, 4):
+        own(a).wait()
 
     for j in range(wd3):
         for i0 in range(0, h3, 8):
@@ -292,6 +306,14 @@
         for a in range(2):
             twice[pl.ds(g * 2 * h2 + a, h2, stride=2), :] = blk
 
+    send(n, range(8))
+    for a in (3, 4, 5):
+        send(a, (0, 1))
+        if a == 5:
+            own(a).wait()
+        pack(a, 0)
+        pack(a, 1)
+        send(a, range(2, 8))
     receive(0)
     for c in weights(0):
         c.wait()

time: 30.5 us -> 29.1 us (0.954)
  Pallas kernels: 27.8 us -> 26.7 us
    pallas_call x1, Pallas kernels: 27.8 us -> 26.7 us  [shards(): pl.pallas_call(functools.partial(body_kernel, axes, counts, shapes), out_...]
where the time goes in v4:
time: 29.1 us; the launch traced here: 29 us
  Pallas kernels  26.7 us (92%)
  local copies, waits for them, and re-layouts  2.26 us (8%)
    pallas_call x1, Pallas kernels, shards(): pl.pallas_call(functools.partial(body_kernel, axes, counts, shapes), out_...  26.7 us
    unnamed x1, local copies, waits for them, and re-layouts  2.26 us

profile of v4, /device:TPU:11, one launch (start us, length us, event | category | flops | bytes accessed | tf_op | source)
XLA Modules:
  0.0 29.0 jit_solution(16968474406367065584)
XLA Ops:
  0.0 26.7 %body.1 = bf16[64,8192]{1,0:T(8,128)(2,1)} custom-call(bf16[16,32,256]{2,1,0:T(8,128)(2,1)} %refs_0_.1, bf16[16,32,256]{2,1,0:T(8,128)(2,1)} %refs_1_.1, bf16[16,32,256]{2,1,0:T(8,128)(2,1)} %refs_2_.1, bf16[16,32,256]{2,1,0:T(8,128)(2,1)} %refs_3_.1, bf16[32,64,128]{2,1,0:T(8,128)(2,1)} %refs_4_.1, bf16[32,64,128]{2,1,0:T(8,128)(2,1)} %refs_5_.1, ...), custom_call_target="tpu_custom_call" | custom-call | tf_op jit(solution)/shard_map/body/pallas_call | solution.py:470
  26.7 2.3 %copy.18 = bf16[64,8192]{1,0:T(8,128)(2,1)} copy(bf16[64,8192]{1,0:T(8,128)(2,1)} %body.1) | data formatting | bytes 2097152

commit v5 on v4

--- a/solution.py
+++ b/solution.py
@@ -403,15 +403,17 @@
     share = wd2 // 8
     parts = []
     for part in range(4):
-        @pl.loop(0, share)
+        @pl.loop(0, share // 2)
         def _(v):
-            g = part * share + v
-            m = twice[pl.ds(pl.multiple_of(g * 2 * h2, 8), 2 * h2), :]
-            turned = pltpu.roll(m, 64, 1)
-            for e in range(2):
-                y = yt[pl.ds(pl.multiple_of((2 * g + e) * 2 * h2, 8), 2 * h2), :]
-                sel = jnp.where(lane_low, m, turned) if e == 0 else jnp.where(lane_low, turned, m)
-                res[:, pl.ds(pl.multiple_of((2 * g + e) * 128, 128), 128)] = jnp.where(sel == want, y, 0.0).astype(BF16)
+            for u in range(2):
+                g = part * share + 2 * v + u
+                m = twice[pl.ds(pl.multiple_of(g * 2 * h2, 8), 2 * h2), :]
+                turned = pltpu.roll(m, 64, 1)
+                for e in range(2):
+                    y = yt[pl.ds(pl.multiple_of((2 * g + e) * 2 * h2, 8), 2 * h2), :]
+                    sel = jnp.where(lane_low, m, turned) if e == 0 else jnp.where(lane_low, turned, m)
+                    to = pl.ds(pl.multiple_of((2 * g + e) * 128, 128), 128)
+                    res[:, to] = jnp.where(sel == want, y, 0.0).astype(BF16)
 
         lanes = slice(part * share * 256, (part + 1) * share * 256)
         parts.append(pltpu.make_async_copy(res.at[:, lanes], out.at[:, lanes], out_sem.at[part]))

time: 29.1 us -> 28 us (0.962)
  Pallas kernels: 26.7 us -> 25.6 us
    pallas_call x1, Pallas kernels: 26.7 us -> 25.6 us  [shards(): pl.pallas_call(functools.partial(body_kernel, axes, counts, shapes), out_...]
where the time goes in v5:
time: 28 us; the launch traced here: 27.8 us
  Pallas kernels  25.6 us (91%)
  local copies, waits for them, and re-layouts  2.26 us (8%)
    pallas_call x1, Pallas kernels, shards(): pl.pallas_call(functools.partial(body_kernel, axes, counts, shapes), out_...  25.6 us
    unnamed x1, local copies, waits for them, and re-layouts  2.26 us

profile of v5, /device:TPU:11, one launch (start us, length us, event | category | flops | bytes accessed | tf_op | source)
XLA Modules:
  0.0 27.8 jit_solution(13957323056443848004)
XLA Ops:
  0.0 25.6 %body.1 = bf16[64,8192]{1,0:T(8,128)(2,1)} custom-call(bf16[16,32,256]{2,1,0:T(8,128)(2,1)} %refs_0_.1, bf16[16,32,256]{2,1,0:T(8,128)(2,1)} %refs_1_.1, bf16[16,32,256]{2,1,0:T(8,128)(2,1)} %refs_2_.1, bf16[16,32,256]{2,1,0:T(8,128)(2,1)} %refs_3_.1, bf16[32,64,128]{2,1,0:T(8,128)(2,1)} %refs_4_.1, bf16[32,64,128]{2,1,0:T(8,128)(2,1)} %refs_5_.1, ...), custom_call_target="tpu_custom_call" | custom-call | tf_op jit(solution)/shard_map/body/pallas_call | solution.py:472
  25.6 2.3 %copy.18 = bf16[64,8192]{1,0:T(8,128)(2,1)} copy(bf16[64,8192]{1,0:T(8,128)(2,1)} %body.1) | data formatting | bytes 2097152
